TPU v7x, 32 devices: a whole 2x2x4 slice. The times are simulated.
32 devices in a mesh: groups: 2 (over y), ep: 8 (over z, x), tp: 2 (over core).
Axes of the slice: x: 2, y: 2, z: 4, core: 2. Of those that a mesh axis runs over, the one named last changes fastest.
Arguments:
- hidden: bfloat16 [128, 4096], P(('groups', 'ep', 'tp')), parts along dimension 0, may hold values from -6 to 6
- norm_gain: float32 [4096], replicated, may hold values from 0.5 to 1.5
- rot_left: float32 [64, 64], replicated, may hold values from -0.75 to 0.75
- rot_right: float32 [64, 64], replicated, may hold values from -0.75 to 0.75
- expert_ids: int32 [128, 8], P(('groups', 'ep')), parts along dimension 0, may hold values from 0 to 63, as said below
- gate_weights: float32 [128, 8], P(('groups', 'ep')), parts along dimension 0, may hold values from 0.05 to 1
- w_gate: bfloat16 [128, 4096, 384], P('ep', 'tp'), may hold values from -0.09375 to 0.09375
- w_up: bfloat16 [128, 4096, 384], P('ep', 'tp'), may hold values from -0.09375 to 0.09375
- w_down: bfloat16 [128, 384, 4096], P('ep', None, 'tp'), may hold values from -0.21875 to 0.21875
- unit_scales: float32 [128, 2, 384], P('ep'), may hold values from 0.25 to 1.75
Outputs:
- moe_out: bfloat16 [128, 4096], P(('groups', 'ep', 'tp')), parts along dimension 0
There are 2 independent parts, one for each index of `groups`. A program takes and returns all parts, laid end to end along the dimension named above; an argument that names none is the same for every part. Nothing has to cross between parts.
Inputs may be any that keep to these rules, and one draw needn't show every extreme that they name: `expert_ids`: each row names 8 different experts. In each aligned block of 8 rows (the rows of one index of ep) no expert is named by more than 2 rows, and in every block some experts are named by exactly 2 rows; every expert is named by exactly 2 rows in some block.
All inputs are finite; a program needn't handle non-finite values.
Results may differ from a plain program's by a relative error of at most 0.0082.
Values may be sent and summed in bfloat16 or wider, within the bound.
No kernel may reach another device: no remote copies, remote signals or barrier semaphores. Data moves between devices by JAX's collectives and lax.ppermute only.
A program may use at most 128 MiB of HBM per device.

v0:
```python
import jax
import jax.numpy as jnp
from jax import lax
from jax.sharding import PartitionSpec as P

EXPERTS = 64


def rotate(hidden, norm_gain, rot_left, rot_right):
    values = hidden.astype(jnp.float32)
    mean_square = jnp.mean(values * values, axis=1, keepdims=True)
    normed = values * lax.rsqrt(mean_square + 1e-06) * norm_gain[None, :]
    factor = rot_left.shape[0]
    square = normed.reshape(-1, factor, factor)
    turned = jnp.einsum("ij,rjk->rik", rot_left, square, precision=lax.Precision.HIGHEST)
    turned = jnp.einsum("rik,lk->ril", turned, rot_right, precision=lax.Precision.HIGHEST)
    return turned.reshape(normed.shape).astype(jnp.bfloat16)


def activate(gate_sum, up_sum, unit_scales):
    gate_scale = unit_scales[None, :, 0, None, :]
    up_scale = unit_scales[None, :, 1, None, :]
    return (jax.nn.silu(gate_sum * gate_scale) * (up_sum * up_scale)).astype(jnp.bfloat16)


def body(
    hidden,
    norm_gain,
    rot_left,
    rot_right,
    expert_ids,
    gate_weights,
    w_gate,
    w_up,
    w_down,
    unit_scales,
):
    ep_count = lax.axis_size("ep")
    group_rows = expert_ids.shape[0]
    top_count = expert_ids.shape[1]
    held_halves = w_gate.shape[0]
    capacity = 5 * group_rows * top_count // (2 * EXPERTS)
    rotated = rotate(hidden, norm_gain, rot_left, rot_right)
    pair_rows = lax.all_to_all(rotated, "tp", split_axis=1, concat_axis=0, tiled=True)
    weight_norm = (gate_weights / jnp.sum(gate_weights, axis=1, keepdims=True)).astype(jnp.bfloat16)
    onehot = (
        expert_ids.reshape(-1)[:, None] == jnp.arange(EXPERTS, dtype=jnp.int32)[None, :]
    ).astype(jnp.int32)
    slot_rank = jnp.sum((jnp.cumsum(onehot, axis=0) - onehot) * onehot, axis=1).reshape(
        group_rows, top_count
    )
    low_target = expert_ids * capacity + slot_rank
    targets = (low_target, low_target + EXPERTS * capacity)
    line_count = 2 * EXPERTS * capacity
    line_index = jnp.arange(line_count, dtype=jnp.int32)[:, None, None]
    matches = jnp.zeros((line_count, group_rows, top_count), jnp.float32)
    for target in targets:
        matches = matches + (line_index == target[None, :, :]).astype(jnp.float32)
    dispatch = jnp.sum(matches, axis=2).astype(jnp.bfloat16)
    outgoing = jnp.dot(dispatch, pair_rows, preferred_element_type=jnp.float32).astype(jnp.bfloat16)
    outgoing = outgoing.reshape(ep_count, held_halves * capacity, -1)
    received = lax.all_to_all(outgoing, "ep", split_axis=0, concat_axis=0, tiled=True)
    received = received.reshape(ep_count, held_halves, capacity, -1)
    gate_sum = jnp.einsum("shcd,hdf->shcf", received, w_gate, preferred_element_type=jnp.float32)
    up_sum = jnp.einsum("shcd,hdf->shcf", received, w_up, preferred_element_type=jnp.float32)
    gate_sum, up_sum = (
        lax.psum_scatter(gate_sum, "tp", scatter_dimension=0, tiled=True),
        lax.psum_scatter(up_sum, "tp", scatter_dimension=0, tiled=True),
    )
    half_hidden = activate(gate_sum, up_sum, unit_scales)
    hidden_units = lax.all_gather(half_hidden, "tp", axis=0, tiled=True)
    partial_value = jnp.einsum(
        "shcf,hfd->shcd", hidden_units, w_down, preferred_element_type=jnp.float32
    ).astype(jnp.bfloat16)
    flat_partial = partial_value.reshape(ep_count, held_halves * capacity, -1)
    returned = lax.all_to_all(flat_partial, "ep", split_axis=0, concat_axis=0, tiled=True)
    returned = returned.reshape(2 * EXPERTS * capacity, -1)
    expert_out = (
        returned[: EXPERTS * capacity].astype(jnp.float32)
        + returned[EXPERTS * capacity :].astype(jnp.float32)
    ).astype(jnp.bfloat16)
    line_spot = (expert_ids * capacity + slot_rank)[:, :, None]
    out_lines = EXPERTS * capacity
    columns = jnp.arange(out_lines, dtype=jnp.int32)[None, None, :]
    hits = (columns == line_spot).astype(jnp.float32)
    mixing = jnp.sum(weight_norm.astype(jnp.float32)[:, :, None] * hits, axis=1).astype(
        jnp.bfloat16
    )
    combined = jnp.dot(mixing, expert_out, preferred_element_type=jnp.float32).astype(jnp.bfloat16)
    return lax.all_to_all(combined, "tp", split_axis=0, concat_axis=1, tiled=True)


def solution(mesh):
    placed = (
        P(("groups", "ep", "tp"), None),
        P(),
        P(),
        P(),
        P(("groups", "ep"), None),
        P(("groups", "ep"), None),
        P("ep", "tp", None),
        P("ep", "tp", None),
        P("ep", None, "tp"),
        P("ep", None, None),
    )
    return jax.shard_map(
        body, mesh=mesh, in_specs=placed, out_specs=P(("groups", "ep", "tp"), None), check_vma=False
    )
```

profile of v0, /device:TPU:0, one launch (start us, length us, event | category | flops | bytes accessed | tf_op | source)
XLA Modules:
  0.0 139.3 jit_solution(9439551862724553802)
XLA Ops:
  6.5 0.9 fusion.16
  7.5 0.8 fusion.17
  8.4 0.4 convolution_bitcast_fusion
  8.8 1.1 convolution_convert_fusion.2
  10.1 0.6 copy.32
  10.7 3.3 %all-to-all-start = ((bf16[4,2,2048]{2,0,1:T(4,128)(2,1)}), bf16[4,2,2048]{2,0,1:T(4,128)(2,1)S(1)}, u32[]{:S(2)}, u32[]{:S(2)}) async-start(bf16[4,2,2048]{2,0,1:T(4,128)(2,1)} %copy.32), calls=%async_computation | async-start | bytes 65536 | tf_op jit(solution)/shard_map/all_to_all | solution.py:44
  14.1 0.8 eq.27
  15.3 0.7 broadcast_add_fusion
  16.1 0.5 convolution_convert_fusion
  16.6 33.4 %all_to_all.45 = bf16[8,32,2048]{2,1,0:T(8,128)(2,1)S(1)} all-to-all(bf16[8,32,2048]{2,1,0:T(8,128)(2,1)S(1)} %bitcast.58), channel_id=1, replica_groups=mesh['groups'=2,'ep'=8,'tp'=2] {'ep'}, dimensions={0} | all-to-all | bytes 2097152 | tf_op jit(solution)/shard_map/all_to_all | solution.py:62
  50.0 0.6 copy.33
  50.6 9.9 %fusion.9 = f32[8,16,2,384]{3,0,2,1:T(8,128)S(1)} fusion(bf16[8,16,2,2048]{3,0,2,1:T(8,128)(2,1)S(1)} %bitcast.55, bf16[16,2048,384]{2,1,0:T(8,128)(2,1)} %param.16), kind=kOutput, calls=%fused_computation.9 | convolution fusion | flops 402653184 | bytes 26607616 | tf_op jit(solution)/shard_map/shcd,hdf->shcf/dot_general | solution.py:64
  60.5 0.9 copy.34
  61.4 10.1 %fusion.12 = f32[8,16,2,384]{3,0,2,1:T(8,128)S(1)} fusion(bf16[8,16,2,2048]{3,0,2,1:T(8,128)(2,1)S(1)} %bitcast.56, bf16[16,2048,384]{2,1,0:T(8,128)(2,1)} %param.17), kind=kOutput, calls=%fused_computation.10 | convolution fusion | flops 402653184 | bytes 26607616 | tf_op jit(solution)/shard_map/shcd,hdf->shcf/dot_general | solution.py:65
  71.6 0.9 copy.36
  72.6 7.1 %reduce-scatter.5.cloned.1.call-done = f32[4,16,2,384]{3,1,2,0:T(8,128)} async-done(((f32[8,16,2,384]{3,1,2,0:T(8,128)}), f32[4,16,2,384]{3,1,2,0:T(8,128)}) %reduce-scatter.5.cloned.1.call-update) | async-done | bytes 196624 | tf_op jit(solution)/shard_map/reduce_scatter | solution.py:68
  79.6 1.1 multiply_convert_fusion
  80.7 1.9 %all_gather.3 = bf16[8,16,2,384]{3,1,2,0:T(8,128)(2,1)S(1)} all-gather(bf16[4,16,2,384]{3,1,2,0:T(8,128)(2,1)S(1)} %multiply_convert_fusion), channel_id=1, replica_groups=mesh['groups'=2,'ep'=8,'tp'=2] {'tp'}, dimensions={0}, use_global_device_ids=true | all-gather | bytes 294912 | tf_op jit(solution)/shard_map/all_gather | solution.py:71
  82.7 11.5 %fusion.6 = bf16[16,8,2,2048]{3,1,2,0:T(8,128)(2,1)S(1)} fusion(bf16[16,384,2048]{2,1,0:T(8,128)(2,1)} %param.18, bf16[8,16,2,384]{3,1,2,0:T(8,128)(2,1)S(1)} %all_gather.3), kind=kOutput, calls=%fused_computation.6 | convolution fusion | flops 403177472 | bytes 26411008 | tf_op jit(solution)/shard_map/shcf,hfd->shcd/dot_general | solution.py:72
  94.2 1.6 %copy.39 = bf16[8,32,2048]{2,1,0:T(8,128)(2,1)} copy(bf16[8,32,2048]{2,0,1:T(8,128)(2,1)S(1)} %bitcast.57) | data formatting | bytes 2097152 | tf_op jit(solution)/shard_map/reshape | solution.py:75
  95.8 5.7 %all-to-all-start.2 = ((bf16[8,32,2048]{2,1,0:T(8,128)(2,1)}), bf16[8,32,2048]{2,1,0:T(8,128)(2,1)S(1)}, u32[]{:S(2)}, u32[]{:S(2)}) async-start(bf16[8,32,2048]{2,1,0:T(8,128)(2,1)} %copy.39), calls=%async_computation.4 | async-start | bytes 2097152 | tf_op jit(solution)/shard_map/all_to_all | solution.py:76
  101.8 26.0 %all-to-all-done.2 = bf16[8,32,2048]{2,1,0:T(8,128)(2,1)S(1)} async-done(((bf16[8,32,2048]{2,1,0:T(8,128)(2,1)}), bf16[8,32,2048]{2,1,0:T(8,128)(2,1)S(1)}, u32[]{:S(2)}, u32[]{:S(2)}) %all-to-all-start.2) | async-done | bytes 1048608 | tf_op jit(solution)/shard_map/all_to_all | solution.py:76
  128.1 3.7 %all_to_all.46 = bf16[2,4,2048]{2,1,0:T(4,128)(2,1)S(1)} all-to-all(bf16[2,4,2048]{2,1,0:T(4,128)(2,1)S(1)} %all_to_all.37), channel_id=1, replica_groups=mesh['groups'=2,'ep'=8,'tp'=2] {'tp'}, dimensions={0} | all-to-all | bytes 65536 | tf_op jit(solution)/shard_map/all_to_all | solution.py:90
  131.9 0.6 copy.53
  (31 shorter events, 1.6 us)
Async XLA Ops:
  6.5 1.9 %copy-start = (f32[64,64]{1,0:T(8,128)S(1)}, f32[64,64]{1,0:T(8,128)}, u32[]{:S(2)}) copy-start(f32[64,64]{1,0:T(8,128)} %param.12) | copy-start | bytes 49156
  10.7 5.2 %all-to-all-start = ((bf16[4,2,2048]{2,0,1:T(4,128)(2,1)}), bf16[4,2,2048]{2,0,1:T(4,128)(2,1)S(1)}, u32[]{:S(2)}, u32[]{:S(2)}) async-start(bf16[4,2,2048]{2,0,1:T(4,128)(2,1)} %copy.32), calls=%async_computation | async-start | bytes 65536 | tf_op jit(solution)/shard_map/all_to_all | solution.py:44
  14.0 58.5 %reduce-scatter.3.cloned.1.call-start = ((), (), s32[]{:S(2)}) async-start(), calls=%async_computation.6 | async-start | bytes 589824 | tf_op jit(solution)/shard_map/reduce_scatter | solution.py:67
  50.6 21.9 %copy-start.2 = (f32[16,2,384]{2,1,0:T(2,128)S(1)}, f32[16,2,384]{2,1,0:T(2,128)}, u32[]{:S(2)}) copy-start(f32[16,2,384]{2,1,0:T(2,128)} %param.19) | copy-start | bytes 147460
  61.4 18.3 %reduce-scatter.5.cloned.1.call-start = ((), (), s32[]{:S(2)}) async-start(), calls=%async_computation.7 | async-start | bytes 589824 | tf_op jit(solution)/shard_map/reduce_scatter | solution.py:68
  61.4 71.1 %copy-start.1 = (f32[64,64]{1,0:T(8,128)S(1)}, f32[64,64]{1,0:T(8,128)}, u32[]{:S(2)}) copy-start(f32[64,64]{1,0:T(8,128)} %param.12) | copy-start | bytes 49156
  71.6 30.0 %copy-start.3 = (f32[8,8]{1,0:T(8,128)S(1)}, f32[8,8]{1,0:T(8,128)}, u32[]{:S(2)}) copy-start(f32[8,8]{1,0:T(8,128)} %param.15) | copy-start | bytes 772
  95.8 32.0 %all-to-all-start.2 = ((bf16[8,32,2048]{2,1,0:T(8,128)(2,1)}), bf16[8,32,2048]{2,1,0:T(8,128)(2,1)S(1)}, u32[]{:S(2)}, u32[]{:S(2)}) async-start(bf16[8,32,2048]{2,1,0:T(8,128)(2,1)} %copy.39), calls=%async_computation.4 | async-start | bytes 2097152 | tf_op jit(solution)/shard_map/all_to_all | solution.py:76
Sparse Core Ops, SparseCore 0:
  61.5 6.8 reduce-scatter.2
  72.6 7.0 reduce-scatter.4
where the time goes:
time: 140 us; the launch traced here: 139 us
  blocking collectives  39.1 us (28%)
  matrix products  33.7 us (24%)
  waiting for transfers between devices  33.1 us (24%)
  between operations  13.6 us (10%)
  starting transfers between devices  9.08 us (6%)
  local copies, waits for them, and re-layouts  6.33 us (5%)
  other arithmetic  4.44 us (3%)
    all_to_all x1, blocking collectives, body(): lax.all_to_all(outgoing, 'ep', split_axis=0, concat_axis=0, tiled=True)  33.4 us
    all_to_all x1, waiting for transfers between devices, body(): lax.all_to_all(flat_partial, 'ep', split_axis=0, concat_axis=0, tiled=True)  26 us
    dot_general x1, matrix products, body(): jnp.einsum('shcf,hfd->shcd', hidden_units, w_down, preferred_element_type...  11.5 us
    dot_general x1, matrix products, body(): jnp.einsum('shcd,hdf->shcf', received, w_up, preferred_element_type=jnp.f...  10.1 us
    dot_general x1, matrix products, body(): jnp.einsum('shcd,hdf->shcf', received, w_gate, preferred_element_type=jnp...  9.91 us
    reduce_scatter x1, waiting for transfers between devices, body(): lax.psum_scatter(up_sum, 'tp', scatter_dimension=0, tiled=True)  7.08 us
    all_to_all x1, starting transfers between devices, body(): lax.all_to_all(flat_partial, 'ep', split_axis=0, concat_axis=0, tiled=True)  5.74 us
    all_to_all x1, blocking collectives, body(): lax.all_to_all(combined, 'tp', split_axis=0, concat_axis=1, tiled=True)  3.75 us
  transfers between devices with their start and end apart: 4, of which 2 were waited for; matrix products, arithmetic and copies ran while one was open for 9% of the time, Pallas kernels for 0%

commit v1 on v0

v1 whole, which is shorter than its diff:
```python
import jax
import jax.numpy as jnp
from jax import lax
from jax.sharding import PartitionSpec as P

META = 128


def rotate(hidden, norm_gain, rot_left, rot_right):
    values = hidden.astype(jnp.float32)
    mean_square = jnp.mean(values * values, axis=1, keepdims=True)
    normed = values * lax.rsqrt(mean_square + 1e-06) * norm_gain[None, :]
    factor = rot_left.shape[0]
    square = normed.reshape(-1, factor, factor)
    turned = jnp.einsum("ij,rjk->rik", rot_left, square, precision=lax.Precision.HIGHEST)
    turned = jnp.einsum("rik,lk->ril", turned, rot_right, precision=lax.Precision.HIGHEST)
    return turned.reshape(normed.shape).astype(jnp.bfloat16)


def body(
    hidden,
    norm_gain,
    rot_left,
    rot_right,
    expert_ids,
    gate_weights,
    w_gate,
    w_up,
    w_down,
    unit_scales,
):
    ep_count = lax.axis_size("ep")
    tp_count = lax.axis_size("tp")
    tp_index = lax.axis_index("tp")
    peers = ep_count * tp_count
    own_rows, width = hidden.shape
    part_width = width // tp_count
    group_rows, top_count = expert_ids.shape
    held_halves, _, half_ff = w_gate.shape
    experts = held_halves * ep_count // 2
    capacity = 5 * group_rows * top_count // (2 * experts)
    slots = capacity * ep_count
    all_rows = peers * own_rows

    rotated = rotate(hidden, norm_gain, rot_left, rot_right)
    weight_norm = (gate_weights / jnp.sum(gate_weights, axis=1, keepdims=True)).astype(jnp.bfloat16)
    meta = jnp.concatenate((expert_ids.astype(jnp.bfloat16), weight_norm), axis=1)
    meta = lax.dynamic_slice_in_dim(meta, tp_index * own_rows, own_rows, axis=0)
    meta = jnp.pad(meta, ((0, 0), (0, META - 2 * top_count)))
    halves = rotated.reshape(own_rows, tp_count, part_width).transpose(1, 0, 2)
    halves = jnp.concatenate(
        (halves, jnp.broadcast_to(meta[None], (tp_count, own_rows, META))), axis=2
    )
    outgoing = jnp.broadcast_to(halves[None], (ep_count,) + halves.shape)
    outgoing = outgoing.reshape(peers, own_rows, part_width + META)
    received = lax.all_to_all(outgoing, ("ep", "tp"), split_axis=0, concat_axis=0, tiled=True)
    received = received.reshape(all_rows, part_width + META)
    rows = received[:, :part_width]
    row_ids = received[:, part_width : part_width + top_count].astype(jnp.int32)
    row_weights = received[:, part_width + top_count : part_width + 2 * top_count].astype(
        jnp.float32
    )

    held = (
        lax.axis_index("ep") * held_halves + jnp.arange(held_halves, dtype=jnp.int32)
    ) % experts
    named = row_ids.T[None, :, :] == held[:, None, None]
    member = jnp.sum(named.astype(jnp.float32), axis=1)
    weight = jnp.sum(jnp.where(named, row_weights.T[None, :, :], 0.0), axis=1)
    rank = jnp.cumsum(member, axis=1) - member
    slot_index = jnp.arange(slots, dtype=jnp.float32)[None, :, None]
    select = (member[:, None, :] > 0) & (rank[:, None, :] == slot_index)
    spread = jnp.where(select, weight[:, None, :], 0.0).astype(jnp.bfloat16)
    inputs = jnp.dot(
        select.astype(jnp.bfloat16).reshape(held_halves * slots, all_rows),
        rows,
        preferred_element_type=jnp.float32,
    ).astype(jnp.bfloat16)
    inputs = inputs.reshape(held_halves, slots, part_width)
    gate_part = jnp.einsum("hsd,hdf->hsf", inputs, w_gate, preferred_element_type=jnp.float32)
    up_part = jnp.einsum("hsd,hdf->hsf", inputs, w_up, preferred_element_type=jnp.float32)
    swap = [(i, i ^ 1) for i in range(tp_count)]
    gate_other = lax.ppermute(gate_part.astype(jnp.bfloat16), "tp", swap)
    up_other = lax.ppermute(up_part.astype(jnp.bfloat16), "tp", swap)
    gate_sum = (gate_part + gate_other.astype(jnp.float32)) * unit_scales[:, 0, None, :]
    up_sum = (up_part + up_other.astype(jnp.float32)) * unit_scales[:, 1, None, :]
    units = (jax.nn.silu(gate_sum) * up_sum).astype(jnp.bfloat16)
    down = jnp.einsum("hsf,hfd->hsd", units, w_down, preferred_element_type=jnp.float32)
    down = down.astype(jnp.bfloat16).reshape(held_halves * slots, part_width)
    combined = lax.dot_general(
        spread.reshape(held_halves * slots, all_rows),
        down,
        (((0,), (0,)), ((), ())),
        preferred_element_type=jnp.float32,
    ).astype(jnp.bfloat16)
    returned = lax.all_to_all(
        combined.reshape(peers, own_rows, part_width),
        ("ep", "tp"),
        split_axis=0,
        concat_axis=0,
        tiled=True,
    )
    returned = returned.reshape(ep_count, tp_count, own_rows, part_width)
    total = jnp.sum(returned.astype(jnp.float32), axis=0)
    return total.transpose(1, 0, 2).reshape(own_rows, width).astype(jnp.bfloat16)


def solution(mesh):
    placed = (
        P(("groups", "ep", "tp"), None),
        P(),
        P(),
        P(),
        P(("groups", "ep"), None),
        P(("groups", "ep"), None),
        P("ep", "tp", None),
        P("ep", "tp", None),
        P("ep", None, "tp"),
        P("ep", None, None),
    )
    return jax.shard_map(
        body, mesh=mesh, in_specs=placed, out_specs=P(("groups", "ep", "tp"), None), check_vma=False
    )
```

time: 140 us -> 71.7 us (0.51)
  blocking collectives: 39.1 us -> 12.9 us
  waiting for transfers between devices: 33.1 us -> 10.3 us
  between operations: 13.6 us -> 0.12 us
  local copies, waits for them, and re-layouts: 6.33 us -> 2.37 us
  matrix products: 33.7 us -> 31.9 us
    all_to_all x2 -> x1, blocking collectives: 37.2 us -> 12.9 us  [body(): lax.all_to_all(combined.reshape(peers, own_rows, part_width), ('ep', 'tp'...]
    all_to_all x2 -> x1, waiting for transfers between devices: 26 us -> 9.25 us  [body(): lax.all_to_all(outgoing, ('ep', 'tp'), split_axis=0, concat_axis=0, tiled...]
    reduce_scatter x2 -> x0, waiting for transfers between devices: 7.1 us -> none  [the longest x1 7.08 us: body(): lax.psum_scatter(up_sum, 'tp', scatter_dimension=0, tiled=True)]
    all_gather x1 -> x0, blocking collectives: 1.95 us -> none  [body(): hidden_units = lax.all_gather(half_hidden, 'tp', axis=0, tiled=True)]
    dot_general x5 -> x4, matrix products: 32.2 us -> 30.4 us  [the longest x1 10.1 us: body(): lax.dot_general(spread.reshape(held_halves * slots, all_rows), down, (((0...]
    transpose x2, local copies, waits for them, and re-layouts: 1.73 us -> 0.12 us  [the longest x1 0.06 us: body(): weight = jnp.sum(jnp.where(named, row_weights.T[None, :, :], 0.0), axis=1)]
    all_to_all x2 -> x1, starting transfers between devices: 8.99 us -> 7.39 us  [body(): lax.all_to_all(outgoing, ('ep', 'tp'), split_axis=0, concat_axis=0, tiled...]
    reshape x2, local copies, waits for them, and re-layouts: 1.66 us -> 0.17 us  [the longest x1 0.11 us: body(): combined.reshape(peers, own_rows, part_width)]
  transfers between devices with their start and end apart: 4 -> 3, of which waited for: 2 -> 2; matrix products, arithmetic and copies ran while one was open for 9% -> 15% of each run, Pallas kernels for 0% -> 0%
where the time goes in v1:
time: 71.7 us; the launch traced here: 71.1 us
  matrix products  31.9 us (44%)
  blocking collectives  12.9 us (18%)
  waiting for transfers between devices  10.3 us (14%)
  starting transfers between devices  8.03 us (11%)
  other arithmetic  5.42 us (8%)
  local copies, waits for them, and re-layouts  2.37 us (3%)
    all_to_all x1, blocking collectives, body(): lax.all_to_all(combined.reshape(peers, own_rows, part_width), ('ep', 'tp'...  12.9 us
    dot_general x1, matrix products, body(): lax.dot_general(spread.reshape(held_halves * slots, all_rows), down, (((0...  10.1 us
    dot_general x1, matrix products, body(): jnp.einsum('hsd,hdf->hsf', inputs, w_up, preferred_element_type=jnp.float32)  9.93 us
    dot_general x1, matrix products, body(): jnp.einsum('hsd,hdf->hsf', inputs, w_gate, preferred_element_type=jnp.flo...  9.92 us
    all_to_all x1, waiting for transfers between devices, body(): lax.all_to_all(outgoing, ('ep', 'tp'), split_axis=0, concat_axis=0, tiled...  9.25 us
    all_to_all x1, starting transfers between devices, body(): lax.all_to_all(outgoing, ('ep', 'tp'), split_axis=0, concat_axis=0, tiled...  7.39 us
  transfers between devices with their start and end apart: 3, of which 2 were waited for; matrix products, arithmetic and copies ran while one was open for 15% of the time, Pallas kernels for 0%

profile of v1, /device:TPU:0, one launch (start us, length us, event | category | flops | bytes accessed | tf_op | source)
XLA Modules:
  0.0 71.1 jit_solution(2545176584892083983)
XLA Ops:
  0.0 0.8 %reduce_sum.46 = f32[8]{0:T(128)S(1)} reduce(f32[8,8]{1,0:T(8,128)} %param.15, f32[]{:T(128)} %constant.20.clone.1), dimensions={1}, to_apply=%region_1.0 | reduce | flops 56 | bytes 292 | tf_op jit(solution)/shard_map/reduce_sum | solution.py:46
  0.8 0.8 %divide_convert_fusion = bf16[8,8]{1,0:T(8,128)(2,1)S(1)} fusion(f32[8,8]{1,0:T(8,128)} %param.15, f32[8]{0:T(128)S(1)} %reduce_sum.46), kind=kLoop, calls=%fused_computation.37 | loop fusion | flops 128 | bytes 416 | tf_op jit(solution)/shard_map/convert_element_type | solution.py:46
  1.6 0.7 convert_element_type.69
  2.3 0.9 %fusion.12 = f32[4]{0:T(128)S(1)} fusion(bf16[4,4096]{1,0:T(4,128)(2,1)} %param.10), kind=kLoop, calls=%fused_computation.21 | loop fusion | flops 49148 | bytes 32784 | tf_op jit(solution)/shard_map/reduce_sum | solution.py:11
  3.2 0.8 %fusion.13 = f32[4,4096]{1,0:T(4,128)S(1)} fusion(bf16[4,4096]{1,0:T(4,128)(2,1)} %param.10, f32[4096]{0:T(1024)} %param.11, f32[4]{0:T(128)S(1)} %add_rsqrt_fusion), kind=kLoop, calls=%fused_computation.22 | loop fusion | flops 49152 | bytes 114704 | tf_op jit(solution)/shard_map/mul | solution.py:12
  4.0 0.1 reshape.73
  4.2 0.4 convolution_bitcast_fusion
  4.6 1.1 %convolution_convert_fusion.2 = bf16[4,64,64]{2,1,0:T(8,128)(2,1)S(1)} fusion(f32[4,64,64]{1,2,0:T(8,128)S(1)} %convolution_bitcast_fusion, f32[64,64]{1,0:T(8,128)} %param.13), kind=kOutput, calls=%fused_computation.6 | convolution fusion | flops 12599296 | bytes 114688 | tf_op jit(solution)/shard_map/rik,lk->ril/dot_general | solution.py:16
  5.7 0.1 convert_element_type.68
  6.0 0.8 %broadcast_in_dim.25 = bf16[8,2,4,2176]{3,2,1,0:T(4,128)(2,1)} broadcast(bf16[2,4,2176]{2,1,0:T(4,128)(2,1)S(1)} %copy.33), dimensions={1,2,3} | broadcast | bytes 313344 | tf_op jit(solution)/shard_map/broadcast_in_dim | solution.py:54
  6.8 7.4 %all-to-all-start = ((bf16[16,4,2176]{2,1,0:T(4,128)(2,1)}), bf16[16,4,2176]{2,1,0:T(4,128)(2,1)S(1)}, u32[]{:S(2)}, u32[]{:S(2)}) async-start(bf16[16,4,2176]{2,1,0:T(4,128)(2,1)} %bitcast.4), calls=%async_computation | async-start | bytes 557056 | tf_op jit(solution)/shard_map/all_to_all | solution.py:56
  14.3 0.9 %fusion.26 = (f32[16,1,384]{2,1,0:T(1,128)S(1)}, f32[16,1,384]{2,1,0:T(1,128)S(1)}) fusion(f32[16,2,384]{2,1,0:T(2,128)} %param.19), kind=kLoop, calls=%fused_computation.47 | loop fusion | bytes 98304 | tf_op jit(solution)/shard_map/slice | solution.py:85
  15.2 9.3 %all-to-all-done = bf16[16,4,2176]{2,1,0:T(4,128)(2,1)S(1)} async-done(((bf16[16,4,2176]{2,1,0:T(4,128)(2,1)}), bf16[16,4,2176]{2,1,0:T(4,128)(2,1)S(1)}, u32[]{:S(2)}, u32[]{:S(2)}) %all-to-all-start) | async-done | bytes 278560 | tf_op jit(solution)/shard_map/all_to_all | solution.py:56
  24.7 0.1 fusion.15
  24.9 0.2 reduce_window_sum.11
  25.2 0.4 convolution_convert_fusion.1
  25.6 9.9 %fusion.27 = (bf16[16,16,384]{2,1,0:T(8,128)(2,1)S(1)}, f32[16,16,384]{2,1,0:T(8,128)S(1)}) fusion(bf16[16,16,2048]{2,1,0:T(8,128)(2,1)S(1)} %bitcast.41, bf16[16,2048,384]{2,1,0:T(8,128)(2,1)} %param.17), kind=kOutput, calls=%fused_computation.48 | convolution fusion | flops 402751488 | bytes 26804224 | tf_op jit(solution)/shard_map/hsd,hdf->hsf/dot_general | solution.py:81
  35.6 0.2 collective-permute-start.1
  35.7 9.9 %fusion.28 = (bf16[16,16,384]{2,1,0:T(8,128)(2,1)S(1)}, f32[16,16,384]{2,1,0:T(8,128)S(1)}) fusion(bf16[16,16,2048]{2,1,0:T(8,128)(2,1)S(1)} %bitcast.42, bf16[16,2048,384]{2,1,0:T(8,128)(2,1)} %param.16), kind=kOutput, calls=%fused_computation.49 | convolution fusion | flops 402751488 | bytes 26804224 | tf_op jit(solution)/shard_map/hsd,hdf->hsf/dot_general | solution.py:80
  45.7 0.5 collective-permute-start
  46.1 1.1 %collective-permute-done = bf16[16,16,384]{2,1,0:T(8,128)(2,1)S(1)} collective-permute-done((bf16[16,16,384]{2,1,0:T(8,128)(2,1)S(1)}, bf16[16,16,384]{2,1,0:T(8,128)(2,1)S(1)}, u32[]{:S(2)}, u32[]{:S(2)}) %collective-permute-start) | collective-permute-done | bytes 196640 | tf_op jit(solution)/shard_map/ppermute | solution.py:83
  47.2 10.1 %fusion.2 = bf16[64,2048]{1,0:T(8,128)(2,1)S(1)} fusion(bf16[16,384,2048]{2,1,0:T(8,128)(2,1)} %param.18, f32[16,16,384]{2,1,0:T(8,128)S(1)} %get-tuple-element.12, bf16[16,16,384]{2,1,0:T(8,128)(2,1)S(1)} %collective-permute-done.1, f32[16,16,384]{2,1,0:T(8,128)S(1)} %get-tuple-element.14, bf16[16,16,384]{2,1,0:T(8,128)(2,1)S(1)} %collective-permute-done, ...), kind=kOutput, calls=%fused_computation.4 | convolution fusion | flops 471646208 | bytes 26663936 | tf_op jit(solution)/shard_map/dot_general | solution.py:90
  57.4 12.9 %all_to_all.10 = bf16[16,4,2048]{2,1,0:T(4,128)(2,1)S(1)} all-to-all(bf16[16,4,2048]{2,1,0:T(4,128)(2,1)S(1)} %reshape.77), channel_id=1, replica_groups=mesh['groups'=2,'ep'=8,'tp'=2] {'ep','tp'}, dimensions={0} | all-to-all | bytes 524288 | tf_op jit(solution)/shard_map/all_to_all | solution.py:96
  70.3 0.7 %reduce = bf16[2,4,2048]{2,1,0:T(4,128)(2,1)} reduce(bf16[8,2,4,2048]{3,2,1,0:T(4,128)(2,1)S(1)} %bitcast.43, bf16[]{:T(256)} %constant.40.clone.1), dimensions={0}, to_apply=%region_5.6.clone | reduce | flops 114688 | bytes 294914 | tf_op jit(solution)/shard_map/reduce_sum | solution.py:104
  (22 shorter events, 0.8 us)
Async XLA Ops:
  0.0 4.2 %copy-start = (f32[64,64]{1,0:T(8,128)S(1)}, f32[64,64]{1,0:T(8,128)}, u32[]{:S(2)}) copy-start(f32[64,64]{1,0:T(8,128)} %param.12) | copy-start | bytes 49156
  6.8 17.7 %all-to-all-start = ((bf16[16,4,2176]{2,1,0:T(4,128)(2,1)}), bf16[16,4,2176]{2,1,0:T(4,128)(2,1)S(1)}, u32[]{:S(2)}, u32[]{:S(2)}) async-start(bf16[16,4,2176]{2,1,0:T(4,128)(2,1)} %bitcast.4), calls=%async_computation | async-start | bytes 557056 | tf_op jit(solution)/shard_map/all_to_all | solution.py:56
  35.6 10.6 %collective-permute-start.1 = (bf16[16,16,384]{2,1,0:T(8,128)(2,1)S(1)}, bf16[16,16,384]{2,1,0:T(8,128)(2,1)S(1)}, u32[]{:S(2)}, u32[]{:S(2)}) collective-permute-start(bf16[16,16,384]{2,1,0:T(8,128)(2,1)S(1)} %get-tuple-element.11), channel_id=1, source_target_pairs={{0,1},{1,0},{2,3},{3,2},{4,5},{5,4},{6,7},{7,6},{8,9},{9,8},{10,11... | collective-permute-start | bytes 589832 | tf_op jit(solution)/shard_map/ppermute | solution.py:84
  45.7 1.5 %collective-permute-start = (bf16[16,16,384]{2,1,0:T(8,128)(2,1)S(1)}, bf16[16,16,384]{2,1,0:T(8,128)(2,1)S(1)}, u32[]{:S(2)}, u32[]{:S(2)}) collective-permute-start(bf16[16,16,384]{2,1,0:T(8,128)(2,1)S(1)} %get-tuple-element.13), channel_id=1, source_target_pairs={{0,1},{1,0},{2,3},{3,2},{4,5},{5,4},{6,7},{7,6},{8,9},{9,8},{10,11... | collective-permute-start | bytes 589832 | tf_op jit(solution)/shard_map/ppermute | solution.py:83

commit v2 on v1

v2 whole, which is shorter than its diff:
```python
import functools

import jax
import jax.numpy as jnp
from jax import lax
from jax.experimental import pallas as pl
from jax.experimental.pallas import tpu as pltpu
from jax.sharding import PartitionSpec as P

LANES = 128
META = 128
MIB = 1 << 20


def exact_dot(left, right):
    return jnp.dot(
        left, right, precision=lax.Precision.HIGHEST, preferred_element_type=jnp.float32
    )


def prelude_kernel(held_halves, experts, ep_count, tp_count, *refs):
    given, out, held, sems = refs[:6], refs[6], refs[7:13], refs[13]
    copies = [pltpu.make_async_copy(a, b, sems.at[i]) for i, (a, b) in enumerate(zip(given, held))]
    for copy in copies:
        copy.start()
    for copy in copies:
        copy.wait()
    hidden, norm_gain, rot_left, rot_right, ids, weights = held
    own_rows, width = hidden.shape
    factor = rot_left.shape[0]
    tiles = width // LANES
    pack = LANES // factor
    top_count = ids.shape[1]
    values = hidden[...].astype(jnp.float32)
    mean_square = jnp.sum(values * values, axis=1, keepdims=True) / width
    normed = values * lax.rsqrt(mean_square + 1e-06) * norm_gain[...]
    lines = jnp.concatenate(
        [normed[:, t * LANES : (t + 1) * LANES] for t in range(tiles)], axis=0
    )
    right = rot_right[...]
    two = jnp.concatenate([right] * pack, axis=0)
    two = jnp.concatenate([two] * pack, axis=1)
    square = (LANES, LANES)
    line = lax.broadcasted_iota(jnp.int32, square, 0)
    lane = lax.broadcasted_iota(jnp.int32, square, 1)
    two = jnp.where(line // factor == lane // factor, two, 0.0)
    lines = lax.dot_general(
        lines,
        two,
        (((1,), (1,)), ((), ())),
        precision=lax.Precision.HIGHEST,
        preferred_element_type=jnp.float32,
    )
    count = tiles * own_rows
    tall = (count, factor)
    tile_of = lax.broadcasted_iota(jnp.int32, tall, 0) // own_rows
    column = lax.broadcasted_iota(jnp.int32, tall, 1)
    picks = [jnp.where(column == pack * tile_of + p, 1.0, 0.0) for p in range(pack)]
    same_row = (
        lax.broadcasted_iota(jnp.int32, (count, count), 0) % own_rows
        == lax.broadcasted_iota(jnp.int32, (count, count), 1) % own_rows
    )
    chosen = exact_dot(jnp.concatenate(picks, axis=0), rot_left[...])
    turned = jnp.zeros((count, LANES), jnp.float32)
    for p_in in range(pack):
        wide = lax.dot_general(
            chosen,
            picks[p_in],
            (((1,), (1,)), ((), ())),
            precision=lax.Precision.HIGHEST,
            preferred_element_type=jnp.float32,
        )
        for p_out in range(pack):
            block = jnp.where(same_row, wide[p_out * count : (p_out + 1) * count, :], 0.0)
            value = exact_dot(block, lines)
            shift = ((p_out - p_in) * factor) % LANES
            if shift:
                value = pltpu.roll(value, shift, 1)
            turned = turned + jnp.where(
                lax.broadcasted_iota(jnp.int32, (count, LANES), 1) // factor == p_out, value, 0.0
            )
    rotated = jnp.concatenate(
        [turned[t * own_rows : (t + 1) * own_rows, :] for t in range(tiles)], axis=1
    ).astype(jnp.bfloat16)

    gate_weights = weights[...]
    share = (gate_weights / jnp.sum(gate_weights, axis=1, keepdims=True)).astype(jnp.bfloat16)
    both = jnp.concatenate((ids[...].astype(jnp.float32), share.astype(jnp.float32)), axis=1)
    meta = jnp.concatenate(
        [both[t * own_rows : (t + 1) * own_rows, :] for t in range(tp_count)]
        + [jnp.zeros((own_rows, META - 2 * top_count * tp_count), jnp.float32)],
        axis=1,
    )
    spot = lax.broadcasted_iota(jnp.int32, meta.shape, 1) == META - 1
    part_width = width // tp_count
    for e in range(ep_count):
        first = float(e * held_halves % experts)
        tail = jnp.where(spot, first, meta).astype(jnp.bfloat16)
        for t in range(tp_count):
            out[e * tp_count + t, :, :part_width] = rotated[
                :, t * part_width : (t + 1) * part_width
            ]
            out[e * tp_count + t, :, part_width:] = tail


def gate_up_kernel(
    tp_count, top_count, slots, received_ref, w_gate, w_up, part, to_send, spread, inputs
):
    held_halves, part_width, half_ff = w_gate.shape
    peers, own_rows, _ = received_ref.shape
    all_rows = peers * own_rows
    received = received_ref[...].reshape(all_rows, part_width + META)
    meta = received[:, part_width:].astype(jnp.float32).T
    shape = (held_halves, all_rows)
    held = lax.broadcasted_iota(jnp.int32, shape, 0).astype(jnp.float32) + meta[META - 1 :, :]
    group = 2 * top_count
    sender = lax.broadcasted_iota(jnp.int32, (group, all_rows), 1) // own_rows % tp_count
    chosen = meta[:group, :]
    for t in range(1, tp_count):
        chosen = jnp.where(sender == t, meta[t * group : (t + 1) * group, :], chosen)
    member = jnp.zeros(shape, jnp.float32)
    weight = jnp.zeros(shape, jnp.float32)
    for choice in range(top_count):
        named = chosen[choice : choice + 1, :] == held
        member = jnp.where(named, 1.0, member)
        weight = jnp.where(named, chosen[top_count + choice : top_count + choice + 1, :], weight)
    square = (all_rows, all_rows)
    earlier = lax.broadcasted_iota(jnp.int32, square, 0) < lax.broadcasted_iota(
        jnp.int32, square, 1
    )
    rank = jnp.dot(
        member.astype(jnp.bfloat16),
        jnp.where(earlier, 1.0, 0.0).astype(jnp.bfloat16),
        preferred_element_type=jnp.float32,
    )
    rank = jnp.where(member > 0, rank, -1.0)
    slot_index = lax.broadcasted_iota(jnp.int32, (slots, all_rows), 0).astype(jnp.float32)
    selects = []
    for j in range(held_halves):
        select = rank[j : j + 1, :] == slot_index
        selects.append(jnp.where(select, 1.0, 0.0))
        spread[j * slots : (j + 1) * slots, :] = jnp.where(
            select, weight[j : j + 1, :], 0.0
        ).astype(jnp.bfloat16)
    select = jnp.concatenate(selects, axis=0).astype(jnp.bfloat16)
    inputs[...] = jnp.dot(
        select, received[:, :part_width], preferred_element_type=jnp.float32
    ).astype(jnp.bfloat16)
    for j in range(held_halves):
        window = slice(j * slots, (j + 1) * slots)
        rows = inputs[window, :]
        for index, w in enumerate((w_gate, w_up)):
            value = jnp.dot(rows, w[j], preferred_element_type=jnp.float32)
            part[index, window, :] = value
            to_send[index, window, :] = value.astype(jnp.bfloat16)


def down_kernel(slots, part, other, unit_scales, spread, w_down, out, held, lines, sems):
    held_halves = w_down.shape[0]
    copies = [
        pltpu.make_async_copy(w_down.at[j], held.at[j], sems.at[j]) for j in range(held_halves)
    ]
    for copy in copies:
        copy.start()
    for j in range(held_halves):
        window = slice(j * slots, (j + 1) * slots)
        gate = (part[0, window, :] + other[0, window, :].astype(jnp.float32)) * unit_scales[
            j, 0:1, :
        ]
        up = (part[1, window, :] + other[1, window, :].astype(jnp.float32)) * unit_scales[
            j, 1:2, :
        ]
        units = (gate / (1.0 + jnp.exp(-gate)) * up).astype(jnp.bfloat16)
        copies[j].wait()
        lines[window, :] = jnp.dot(
            units, held[j], preferred_element_type=jnp.float32
        ).astype(jnp.bfloat16)
    out[...] = lax.dot_general(
        spread[...], lines[...], (((0,), (0,)), ((), ())), preferred_element_type=jnp.float32
    ).astype(jnp.bfloat16)


def body(
    hidden,
    norm_gain,
    rot_left,
    rot_right,
    expert_ids,
    gate_weights,
    w_gate,
    w_up,
    w_down,
    unit_scales,
):
    ep_count = lax.axis_size("ep")
    tp_count = lax.axis_size("tp")
    peers = ep_count * tp_count
    own_rows, width = hidden.shape
    part_width = width // tp_count
    group_rows, top_count = expert_ids.shape
    held_halves, _, half_ff = w_gate.shape
    experts = held_halves * ep_count // 2
    capacity = 5 * group_rows * top_count // (2 * experts)
    slots = capacity * ep_count
    all_rows = peers * own_rows
    lines = held_halves * slots

    vmem = pl.BlockSpec(memory_space=pltpu.VMEM)
    given = (hidden, norm_gain[None, :], rot_left, rot_right, expert_ids, gate_weights)
    outgoing = pl.pallas_call(
        functools.partial(prelude_kernel, held_halves, experts, ep_count, tp_count),
        out_shape=pltpu.VMEM((peers, own_rows, part_width + META), jnp.bfloat16),
        in_specs=[pl.BlockSpec(memory_space=pltpu.HBM)] * len(given),
        out_specs=vmem,
        scratch_shapes=[pltpu.VMEM(array.shape, array.dtype) for array in given]
        + [pltpu.SemaphoreType.DMA((len(given),))],
        cost_estimate=pl.CostEstimate(flops=1 << 36, bytes_accessed=MIB, transcendentals=0),
        compiler_params=pltpu.CompilerParams(vmem_limit_bytes=4 * MIB),
        name="prelude",
    )(*[pltpu.with_memory_space_constraint(array, pltpu.HBM) for array in given])
    received = lax.all_to_all(outgoing, ("ep", "tp"), split_axis=0, concat_axis=0, tiled=True)
    part, to_send, spread = pl.pallas_call(
        functools.partial(gate_up_kernel, tp_count, top_count, slots),
        out_shape=(
            pltpu.VMEM((2, lines, half_ff), jnp.float32),
            pltpu.VMEM((2, lines, half_ff), jnp.bfloat16),
            pltpu.VMEM((lines, all_rows), jnp.bfloat16),
        ),
        in_specs=[vmem] * 3,
        out_specs=(vmem,) * 3,
        scratch_shapes=[pltpu.VMEM((lines, part_width), jnp.bfloat16)],
        compiler_params=pltpu.CompilerParams(vmem_limit_bytes=5 * MIB),
        name="gate_up",
    )(
        received,
        pltpu.with_memory_space_constraint(w_gate, pltpu.VMEM),
        pltpu.with_memory_space_constraint(w_up, pltpu.VMEM),
    )
    other = lax.ppermute(to_send, "tp", [(i, i ^ 1) for i in range(tp_count)])
    combined = pl.pallas_call(
        functools.partial(down_kernel, slots),
        out_shape=jax.ShapeDtypeStruct((all_rows, part_width), jnp.bfloat16),
        in_specs=[vmem] * 4 + [pl.BlockSpec(memory_space=pltpu.HBM)],
        out_specs=vmem,
        scratch_shapes=[
            pltpu.VMEM(w_down.shape, w_down.dtype),
            pltpu.VMEM((lines, part_width), jnp.bfloat16),
            pltpu.SemaphoreType.DMA((held_halves,)),
        ],
        compiler_params=pltpu.CompilerParams(vmem_limit_bytes=36 * MIB),
        name="down",
    )(part, other, unit_scales, spread, w_down)
    returned = lax.all_to_all(
        combined.reshape(peers, own_rows, part_width),
        ("ep", "tp"),
        split_axis=0,
        concat_axis=0,
        tiled=True,
    )
    returned = returned.reshape(ep_count, tp_count, own_rows, part_width)
    total = jnp.sum(returned.astype(jnp.float32), axis=0)
    return total.transpose(1, 0, 2).reshape(own_rows, width).astype(jnp.bfloat16)


def solution(mesh):
    placed = (
        P(("groups", "ep", "tp"), None),
        P(),
        P(),
        P(),
        P(("groups", "ep"), None),
        P(("groups", "ep"), None),
        P("ep", "tp", None),
        P("ep", "tp", None),
        P("ep", None, "tp"),
        P("ep", None, None),
    )
    return jax.shard_map(
        body, mesh=mesh, in_specs=placed, out_specs=P(("groups", "ep", "tp"), None), check_vma=False
    )
```

time: 71.7 us -> 52.6 us (0.73)
  matrix products: 31.9 us -> 0 us
  Pallas kernels: 0 us -> 19.1 us
  blocking collectives: 12.9 us -> 30.6 us
  waiting for transfers between devices: 10.3 us -> 1.62 us
  starting transfers between devices: 8.03 us -> 0.17 us
  other arithmetic: 5.42 us -> 0.73 us
  local copies, waits for them, and re-layouts: 2.37 us -> 0.12 us
    dot_general x6 -> x0, matrix products: 31.9 us -> none  [the longest x1 10.1 us: body(): lax.dot_general(spread.reshape(held_halves * slots, all_rows), down, (((0...]
    pallas_call x0 -> x3, Pallas kernels: none -> 19.1 us  [the longest x1 8.86 us: body(): pl.pallas_call(functools.partial(down_kernel, slots), out_shape=jax.Shape...]
    all_to_all x0 -> x1, blocking collectives: none -> 17.8 us  [body(): lax.all_to_all(outgoing, ('ep', 'tp'), split_axis=0, concat_axis=0, tiled...]
    all_to_all x1 -> x0, waiting for transfers between devices: 9.25 us -> none  [body(): lax.all_to_all(outgoing, ('ep', 'tp'), split_axis=0, concat_axis=0, tiled...]
    all_to_all x1 -> x0, starting transfers between devices: 7.39 us -> none  [body(): lax.all_to_all(outgoing, ('ep', 'tp'), split_axis=0, concat_axis=0, tiled...]
    reduce_sum x3 -> x0, other arithmetic: 1.85 us -> none  [the longest x1 0.9 us: rotate(): mean_square = jnp.mean(values * values, axis=1, keepdims=True)]
    convert_element_type x2 -> x0, other arithmetic: 1.45 us -> none  [the longest x1 0.76 us: body(): (gate_weights / jnp.sum(gate_weights, axis=1, keepdims=True)).astype(jnp....]
    slice x1 -> x0, local copies, waits for them, and re-layouts: 0.92 us -> none  [body(): unit_scales[:, 0, None, :]]
  transfers between devices with their start and end apart: 3 -> 1, of which waited for: 2 -> 1; matrix products, arithmetic and copies ran while one was open for 15% -> 0% of each run, Pallas kernels for 0% -> 0%
where the time goes in v2:
time: 52.6 us; the launch traced here: 52.4 us
  blocking collectives  30.6 us (58%)
  Pallas kernels  19.1 us (36%)
  waiting for transfers between devices  1.62 us (3%)
  other arithmetic  0.73 us (1%)
    all_to_all x1, blocking collectives, body(): lax.all_to_all(outgoing, ('ep', 'tp'), split_axis=0, concat_axis=0, tiled...  17.8 us
    all_to_all x1, blocking collectives, body(): lax.all_to_all(combined.reshape(peers, own_rows, part_width), ('ep', 'tp'...  12.8 us
    pallas_call x1, Pallas kernels, body(): pl.pallas_call(functools.partial(down_kernel, slots), out_shape=jax.Shape...  8.86 us
    pallas_call x1, Pallas kernels, body(): pl.pallas_call(functools.partial(gate_up_kernel, tp_count, top_count, slo...  8.12 us
    pallas_call x1, Pallas kernels, body(): pl.pallas_call(functools.partial(prelude_kernel, held_halves, experts, ep...  2.16 us
    ppermute x1, waiting for transfers between devices, body(): other = lax.ppermute(to_send, 'tp', [(i, i ^ 1) for i in range(tp_count)])  1.62 us
  transfers between devices with their start and end apart: 1, of which 1 were waited for; matrix products, arithmetic and copies ran while one was open for 0% of the time, Pallas kernels for 0%

profile of v2, /device:TPU:0, one launch (start us, length us, event | category | flops | bytes accessed | tf_op | source)
XLA Modules:
  0.0 52.4 jit_solution(833505324427040139)
XLA Ops:
  0.0 0.0 copy-start
  0.0 0.0 copy-start.1
  0.0 2.2 %prelude.1 = bf16[16,4,2176]{2,1,0:T(4,128)(2,1)S(1)} custom-call(bf16[4,4096]{1,0:T(4,128)(2,1)} %refs_0_.1, f32[1,4096]{1,0:T(1,128)} %bitcast.6, f32[64,64]{1,0:T(8,128)} %refs_2_.1, f32[64,64]{1,0:T(8,128)} %refs_3_.1, s32[8,8]{1,0:T(8,128)} %refs_4_.1, f32[8,8]{1,0:T(8,128)} %refs_5_.1), custom_call_target="tpu_custom_call" | custom-call | flops 68719476736 | bytes 1048576 | tf_op jit(solution)/shard_map/prelude/pallas_call | solution.py:210
  2.2 17.8 %all_to_all.10.received_ref = bf16[16,4,2176]{2,1,0:T(4,128)(2,1)} all-to-all(bf16[16,4,2176]{2,1,0:T(4,128)(2,1)S(1)} %prelude.1), channel_id=1, replica_groups=mesh['groups'=2,'ep'=8,'tp'=2] {'ep','tp'}, dimensions={0} | all-to-all | bytes 557056 | tf_op jit(solution)/shard_map/all_to_all | solution.py:221
  20.0 0.0 copy-done
  20.0 0.0 copy-done.1
  20.0 0.0 copy-start.2
  20.0 8.1 %gate_up.1 = (f32[2,256,384]{2,1,0:T(8,128)S(1)}, bf16[2,256,384]{2,1,0:T(8,128)(2,1)S(1)}, bf16[256,64]{1,0:T(8,128)(2,1)S(1)}) custom-call(bf16[16,4,2176]{2,1,0:T(4,128)(2,1)} %all_to_all.10.received_ref, bf16[16,2048,384]{2,1,0:T(8,128)(2,1)S(1)} %copy-done, bf16[16,2048,384]{2,1,0:T(8,128)(2,1)S(1)} %copy-done.1), custom_call_target="tpu_custom_call" | custom-call | tf_op jit(solution)/shard_map/gate_up/pallas_call | solution.py:222
  28.1 0.2 collective-permute-start
  28.3 1.6 %collective-permute-done.other = bf16[2,256,384]{2,1,0:T(8,128)(2,1)S(1)} collective-permute-done((bf16[2,256,384]{2,1,0:T(8,128)(2,1)S(1)}, bf16[2,256,384]{2,1,0:T(8,128)(2,1)S(1)}, u32[]{:S(2)}, u32[]{:S(2)}) %collective-permute-start) | collective-permute-done | bytes 393248 | tf_op jit(solution)/shard_map/ppermute | solution.py:239
  29.9 0.0 copy-done.2
  29.9 8.9 %down.1 = bf16[64,2048]{1,0:T(8,128)(2,1)S(1)} custom-call(f32[2,256,384]{2,1,0:T(8,128)S(1)} %get-tuple-element.8.part, bf16[2,256,384]{2,1,0:T(8,128)(2,1)S(1)} %collective-permute-done.other, f32[16,2,384]{2,1,0:T(2,128)S(1)} %copy-done.2, bf16[256,64]{1,0:T(8,128)(2,1)S(1)} %get-tuple-element.10.spread, bf16[16,384,2048]{2,1,0:T(8,128)(2,1)} %w_down.1), custom_call_target="tpu_custom_call" | custom-call | tf_op jit(solution)/shard_map/down/pallas_call | solution.py:240
  38.8 0.1 reshape.8
  38.9 12.8 %all_to_all.11 = bf16[16,4,2048]{2,1,0:T(4,128)(2,1)S(1)} all-to-all(bf16[16,4,2048]{2,1,0:T(4,128)(2,1)S(1)} %reshape.8), channel_id=1, replica_groups=mesh['groups'=2,'ep'=8,'tp'=2] {'ep','tp'}, dimensions={0} | all-to-all | bytes 524288 | tf_op jit(solution)/shard_map/all_to_all | solution.py:253
  51.7 0.7 %reduce = bf16[2,4,2048]{2,1,0:T(4,128)(2,1)} reduce(bf16[8,2,4,2048]{3,2,1,0:T(4,128)(2,1)S(1)} %bitcast.5, bf16[]{:T(256)} %constant.5), dimensions={0}, to_apply=%region_0.0.clone | reduce | flops 114688 | bytes 294914 | tf_op jit(solution)/shard_map/reduce_sum | solution.py:261
Async XLA Ops:
  0.0 20.0 %copy-start = (bf16[16,2048,384]{2,1,0:T(8,128)(2,1)S(1)}, bf16[16,2048,384]{2,1,0:T(8,128)(2,1)}, u32[]{:S(2)}) copy-start(bf16[16,2048,384]{2,1,0:T(8,128)(2,1)} %w_gate.1) | copy-start | bytes 75497472
  0.0 20.0 %copy-start.1 = (bf16[16,2048,384]{2,1,0:T(8,128)(2,1)S(1)}, bf16[16,2048,384]{2,1,0:T(8,128)(2,1)}, u32[]{:S(2)}) copy-start(bf16[16,2048,384]{2,1,0:T(8,128)(2,1)} %w_up.1) | copy-start | bytes 75497472
  20.0 9.9 %copy-start.2 = (f32[16,2,384]{2,1,0:T(2,128)S(1)}, f32[16,2,384]{2,1,0:T(2,128)}, u32[]{:S(2)}) copy-start(f32[16,2,384]{2,1,0:T(2,128)} %unit_scales.1) | copy-start | bytes 147460
  28.1 1.8 %collective-permute-start = (bf16[2,256,384]{2,1,0:T(8,128)(2,1)S(1)}, bf16[2,256,384]{2,1,0:T(8,128)(2,1)S(1)}, u32[]{:S(2)}, u32[]{:S(2)}) collective-permute-start(bf16[2,256,384]{2,1,0:T(8,128)(2,1)S(1)} %get-tuple-element.9), channel_id=1, source_target_pairs={{0,1},{1,0},{2,3},{3,2},{4,5},{5,4},{6,7},{7,6},{8,9},{9,8},{10,11... | collective-permute-start | bytes 1179656 | tf_op jit(solution)/shard_map/ppermute | solution.py:239

commit v3 on v2

--- a/solution.py
+++ b/solution.py
@@ -10,6 +10,7 @@
 LANES = 128
 META = 128
 MIB = 1 << 20
+RING = 7
 
 
 def exact_dot(left, right):
@@ -104,9 +105,16 @@
 
 
 def gate_up_kernel(
-    tp_count, top_count, slots, received_ref, w_gate, w_up, part, to_send, spread, inputs
+    tp_count, top_count, slots, received_ref, w_gate, w_up, part, to_send, spread, inputs, ring, sems
 ):
     held_halves, part_width, half_ff = w_gate.shape
+    depth = ring.shape[0]
+    copies = [
+        pltpu.make_async_copy(w_up.at[j], ring.at[j % depth], sems.at[j % depth])
+        for j in range(held_halves)
+    ]
+    for j in range(depth):
+        copies[j].start()
     peers, own_rows, _ = received_ref.shape
     all_rows = peers * own_rows
     received = received_ref[...].reshape(all_rows, part_width + META)
@@ -146,23 +154,23 @@
     inputs[...] = jnp.dot(
         select, received[:, :part_width], preferred_element_type=jnp.float32
     ).astype(jnp.bfloat16)
-    for j in range(held_halves):
-        window = slice(j * slots, (j + 1) * slots)
-        rows = inputs[window, :]
-        for index, w in enumerate((w_gate, w_up)):
-            value = jnp.dot(rows, w[j], preferred_element_type=jnp.float32)
+    for index in range(2):
+        for j in range(held_halves):
+            window = slice(j * slots, (j + 1) * slots)
+            if index == 0:
+                held_weight = w_gate[j]
+            else:
+                copies[j].wait()
+                held_weight = ring[j % depth]
+            value = jnp.dot(inputs[window, :], held_weight, preferred_element_type=jnp.float32)
             part[index, window, :] = value
             to_send[index, window, :] = value.astype(jnp.bfloat16)
-
-
-def down_kernel(slots, part, other, unit_scales, spread, w_down, out, held, lines, sems):
-    held_halves = w_down.shape[0]
-    copies = [
-        pltpu.make_async_copy(w_down.at[j], held.at[j], sems.at[j]) for j in range(held_halves)
-    ]
-    for copy in copies:
-        copy.start()
-    for j in range(held_halves):
+            if index == 1 and j + depth < held_halves:
+                copies[j + depth].start()
+
+
+def down_kernel(slots, part, other, unit_scales, spread, w_down, out, lines):
+    for j in range(w_down.shape[0]):
         window = slice(j * slots, (j + 1) * slots)
         gate = (part[0, window, :] + other[0, window, :].astype(jnp.float32)) * unit_scales[
             j, 0:1, :
@@ -171,9 +179,8 @@
             j, 1:2, :
         ]
         units = (gate / (1.0 + jnp.exp(-gate)) * up).astype(jnp.bfloat16)
-        copies[j].wait()
         lines[window, :] = jnp.dot(
-            units, held[j], preferred_element_type=jnp.float32
+            units, w_down[j], preferred_element_type=jnp.float32
         ).astype(jnp.bfloat16)
     out[...] = lax.dot_general(
         spread[...], lines[...], (((0,), (0,)), ((), ())), preferred_element_type=jnp.float32
@@ -204,6 +211,7 @@
     slots = capacity * ep_count
     all_rows = peers * own_rows
     lines = held_halves * slots
+    depth = min(RING, held_halves)
 
     vmem = pl.BlockSpec(memory_space=pltpu.VMEM)
     given = (hidden, norm_gain[None, :], rot_left, rot_right, expert_ids, gate_weights)
@@ -226,30 +234,30 @@
             pltpu.VMEM((2, lines, half_ff), jnp.bfloat16),
             pltpu.VMEM((lines, all_rows), jnp.bfloat16),
         ),
-        in_specs=[vmem] * 3,
+        in_specs=[vmem, vmem, pl.BlockSpec(memory_space=pltpu.HBM)],
         out_specs=(vmem,) * 3,
-        scratch_shapes=[pltpu.VMEM((lines, part_width), jnp.bfloat16)],
-        compiler_params=pltpu.CompilerParams(vmem_limit_bytes=5 * MIB),
+        scratch_shapes=[
+            pltpu.VMEM((lines, part_width), jnp.bfloat16),
+            pltpu.VMEM((depth,) + w_up.shape[1:], w_up.dtype),
+            pltpu.SemaphoreType.DMA((depth,)),
+        ],
+        compiler_params=pltpu.CompilerParams(vmem_limit_bytes=13 * MIB),
         name="gate_up",
     )(
         received,
         pltpu.with_memory_space_constraint(w_gate, pltpu.VMEM),
-        pltpu.with_memory_space_constraint(w_up, pltpu.VMEM),
+        pltpu.with_memory_space_constraint(w_up, pltpu.HBM),
     )
     other = lax.ppermute(to_send, "tp", [(i, i ^ 1) for i in range(tp_count)])
     combined = pl.pallas_call(
         functools.partial(down_kernel, slots),
         out_shape=jax.ShapeDtypeStruct((all_rows, part_width), jnp.bfloat16),
-        in_specs=[vmem] * 4 + [pl.BlockSpec(memory_space=pltpu.HBM)],
+        in_specs=[vmem] * 5,
         out_specs=vmem,
-        scratch_shapes=[
-            pltpu.VMEM(w_down.shape, w_down.dtype),
-            pltpu.VMEM((lines, part_width), jnp.bfloat16),
-            pltpu.SemaphoreType.DMA((held_halves,)),
-        ],
-        compiler_params=pltpu.CompilerParams(vmem_limit_bytes=36 * MIB),
+        scratch_shapes=[pltpu.VMEM((lines, part_width), jnp.bfloat16)],
+        compiler_params=pltpu.CompilerParams(vmem_limit_bytes=5 * MIB),
         name="down",
-    )(part, other, unit_scales, spread, w_down)
+    )(part, other, unit_scales, spread, pltpu.with_memory_space_constraint(w_down, pltpu.VMEM))
     returned = lax.all_to_all(
         combined.reshape(peers, own_rows, part_width),
         ("ep", "tp"),

time: 52.6 us -> 51.9 us (0.987)
  Pallas kernels: 19.1 us -> 18.4 us
    pallas_call x1, Pallas kernels: 8.86 us -> 3.57 us  [body(): pl.pallas_call(functools.partial(down_kernel, slots), out_shape=jax.Shape...]
    pallas_call x1, Pallas kernels: 8.12 us -> 12.7 us  [body(): pl.pallas_call(functools.partial(gate_up_kernel, tp_count, top_count, slo...]
where the time goes in v3:
time: 51.9 us; the launch traced here: 51.7 us
  blocking collectives  30.5 us (59%)
  Pallas kernels  18.4 us (35%)
  waiting for transfers between devices  1.61 us (3%)
  other arithmetic  0.73 us (1%)
    all_to_all x1, blocking collectives, body(): lax.all_to_all(outgoing, ('ep', 'tp'), split_axis=0, concat_axis=0, tiled...  17.7 us
    all_to_all x1, blocking collectives, body(): lax.all_to_all(combined.reshape(peers, own_rows, part_width), ('ep', 'tp'...  12.8 us
    pallas_call x1, Pallas kernels, body(): pl.pallas_call(functools.partial(gate_up_kernel, tp_count, top_count, slo...  12.7 us
    pallas_call x1, Pallas kernels, body(): pl.pallas_call(functools.partial(down_kernel, slots), out_shape=jax.Shape...  3.57 us
    pallas_call x1, Pallas kernels, body(): pl.pallas_call(functools.partial(prelude_kernel, held_halves, experts, ep...  2.16 us
    ppermute x1, waiting for transfers between devices, body(): other = lax.ppermute(to_send, 'tp', [(i, i ^ 1) for i in range(tp_count)])  1.61 us
  transfers between devices with their start and end apart: 1, of which 1 were waited for; matrix products, arithmetic and copies ran while one was open for 0% of the time, Pallas kernels for 0%

profile of v3, /device:TPU:0, one launch (start us, length us, event | category | flops | bytes accessed | tf_op | source)
XLA Modules:
  0.0 51.7 jit_solution(11495712116526101795)
XLA Ops:
  0.0 0.0 copy-start
  0.0 0.0 slice-start
  0.0 0.0 slice-start.1
  0.0 0.0 slice-start.2
  0.0 0.0 slice-start.3
  0.0 0.0 slice-start.4
  0.0 2.2 %prelude.1 = bf16[16,4,2176]{2,1,0:T(4,128)(2,1)S(1)} custom-call(bf16[4,4096]{1,0:T(4,128)(2,1)} %refs_0_.1, f32[1,4096]{1,0:T(1,128)} %bitcast.8, f32[64,64]{1,0:T(8,128)} %refs_2_.1, f32[64,64]{1,0:T(8,128)} %refs_3_.1, s32[8,8]{1,0:T(8,128)} %refs_4_.1, f32[8,8]{1,0:T(8,128)} %refs_5_.1), custom_call_target="tpu_custom_call" | custom-call | flops 68719476736 | bytes 1048576 | tf_op jit(solution)/shard_map/prelude/pallas_call | solution.py:218
  2.2 0.0 slice-start.5
  2.2 17.7 %all_to_all.10.received_ref = bf16[16,4,2176]{2,1,0:T(4,128)(2,1)S(1)} all-to-all(bf16[16,4,2176]{2,1,0:T(4,128)(2,1)S(1)} %prelude.1), channel_id=1, replica_groups=mesh['groups'=2,'ep'=8,'tp'=2] {'ep','tp'}, dimensions={0} | all-to-all | bytes 557056 | tf_op jit(solution)/shard_map/all_to_all | solution.py:229
  19.9 0.0 copy-done
  20.0 12.7 %gate_up.1 = (f32[2,256,384]{2,1,0:T(8,128)S(1)}, bf16[2,256,384]{2,1,0:T(8,128)(2,1)S(1)}, bf16[256,64]{1,0:T(8,128)(2,1)S(1)}) custom-call(bf16[16,4,2176]{2,1,0:T(4,128)(2,1)S(1)} %all_to_all.10.received_ref, bf16[16,2048,384]{2,1,0:T(8,128)(2,1)S(1)} %copy-done, bf16[16,2048,384]{2,1,0:T(8,128)(2,1)} %w_up.1), custom_call_target="tpu_custom_call" | custom-call | tf_op jit(solution)/shard_map/gate_up/pallas_call | solution.py:230
  32.6 0.2 collective-permute-start
  32.8 1.6 %collective-permute-done.other = bf16[2,256,384]{2,1,0:T(8,128)(2,1)S(1)} collective-permute-done((bf16[2,256,384]{2,1,0:T(8,128)(2,1)S(1)}, bf16[2,256,384]{2,1,0:T(8,128)(2,1)S(1)}, u32[]{:S(2)}, u32[]{:S(2)}) %collective-permute-start) | collective-permute-done | bytes 393248 | tf_op jit(solution)/shard_map/ppermute | solution.py:251
  34.4 0.0 slice-done
  34.4 0.0 slice-done.1
  34.4 0.0 slice-done.2
  34.4 0.0 slice-done.3
  34.4 0.0 slice-done.4
  34.5 0.0 slice-done.5
  34.5 0.0 copy-done.1
  34.5 3.6 %down.1 = bf16[64,2048]{1,0:T(8,128)(2,1)S(1)} custom-call(f32[2,256,384]{2,1,0:T(8,128)S(1)} %get-tuple-element.8.part, bf16[2,256,384]{2,1,0:T(8,128)(2,1)S(1)} %collective-permute-done.other, f32[16,2,384]{2,1,0:T(2,128)S(1)} %copy-done.1, bf16[256,64]{1,0:T(8,128)(2,1)S(1)} %get-tuple-element.10.spread, bf16[16,384,2048]{2,1,0:T(8,128)(2,1)S(1)} %bitcast.6), custom_call_target="tpu_custom_call" | custom-call | tf_op jit(solution)/shard_map/down/pallas_call | solution.py:252
  38.1 0.1 reshape.8
  38.2 12.8 %all_to_all.11 = bf16[16,4,2048]{2,1,0:T(4,128)(2,1)S(1)} all-to-all(bf16[16,4,2048]{2,1,0:T(4,128)(2,1)S(1)} %reshape.8), channel_id=1, replica_groups=mesh['groups'=2,'ep'=8,'tp'=2] {'ep','tp'}, dimensions={0} | all-to-all | bytes 524288 | tf_op jit(solution)/shard_map/all_to_all | solution.py:261
  50.9 0.7 %reduce = bf16[2,4,2048]{2,1,0:T(4,128)(2,1)} reduce(bf16[8,2,4,2048]{3,2,1,0:T(4,128)(2,1)S(1)} %bitcast.7, bf16[]{:T(256)} %constant.5), dimensions={0}, to_apply=%region_0.0.clone | reduce | flops 114688 | bytes 294914 | tf_op jit(solution)/shard_map/reduce_sum | solution.py:269
  (2 shorter events, 0.0 us)
Async XLA Ops:
  0.0 19.9 %copy-start = (bf16[16,2048,384]{2,1,0:T(8,128)(2,1)S(1)}, bf16[16,2048,384]{2,1,0:T(8,128)(2,1)}, u32[]{:S(2)}) copy-start(bf16[16,2048,384]{2,1,0:T(8,128)(2,1)} %w_gate.1) | copy-start | bytes 75497472
  0.0 34.4 %slice-start = ((s8[25165824]{0:T(1024)(128)(4,1)}), s8[4194304]{0:T(1024)(128)(4,1)S(1)}, s32[]{:S(2)}) async-start(s8[25165824]{0:T(1024)(128)(4,1)} %bitcast.5), calls=%async_computation.2 | async-start | bytes 8388608
  0.0 34.4 %slice-start.1 = ((s8[25165824]{0:T(1024)(128)(4,1)}), s8[4194304]{0:T(1024)(128)(4,1)S(1)}, s32[]{:S(2)}) async-start(s8[25165824]{0:T(1024)(128)(4,1)} %bitcast.5), calls=%async_computation.3 | async-start | bytes 8388608
  0.0 34.4 %slice-start.2 = ((s8[25165824]{0:T(1024)(128)(4,1)}), s8[4194304]{0:T(1024)(128)(4,1)S(1)}, s32[]{:S(2)}) async-start(s8[25165824]{0:T(1024)(128)(4,1)} %bitcast.5), calls=%async_computation.4 | async-start | bytes 8388608
  0.0 34.4 %slice-start.3 = ((s8[25165824]{0:T(1024)(128)(4,1)}), s8[4194304]{0:T(1024)(128)(4,1)S(1)}, s32[]{:S(2)}) async-start(s8[25165824]{0:T(1024)(128)(4,1)} %bitcast.5), calls=%async_computation.5 | async-start | bytes 8388608
  0.0 34.4 %slice-start.4 = ((s8[25165824]{0:T(1024)(128)(4,1)}), s8[4194304]{0:T(1024)(128)(4,1)S(1)}, s32[]{:S(2)}) async-start(s8[25165824]{0:T(1024)(128)(4,1)} %bitcast.5), calls=%async_computation.6 | async-start | bytes 8388608
  2.2 32.3 %slice-start.5 = ((s8[25165824]{0:T(1024)(128)(4,1)}), s8[4194304]{0:T(1024)(128)(4,1)S(1)}, s32[]{:S(2)}) async-start(s8[25165824]{0:T(1024)(128)(4,1)} %bitcast.5), calls=%async_computation.7 | async-start | bytes 8388608
  19.9 14.5 %copy-start.1 = (f32[16,2,384]{2,1,0:T(2,128)S(1)}, f32[16,2,384]{2,1,0:T(2,128)}, u32[]{:S(2)}) copy-start(f32[16,2,384]{2,1,0:T(2,128)} %unit_scales.1) | copy-start | bytes 147460
  32.6 1.8 %collective-permute-start = (bf16[2,256,384]{2,1,0:T(8,128)(2,1)S(1)}, bf16[2,256,384]{2,1,0:T(8,128)(2,1)S(1)}, u32[]{:S(2)}, u32[]{:S(2)}) collective-permute-start(bf16[2,256,384]{2,1,0:T(8,128)(2,1)S(1)} %get-tuple-element.9), channel_id=1, source_target_pairs={{0,1},{1,0},{2,3},{3,2},{4,5},{5,4},{6,7},{7,6},{8,9},{9,8},{10,11... | collective-permute-start | bytes 1179656 | tf_op jit(solution)/shard_map/ppermute | solution.py:251

commit v4 on v3

--- a/solution.py
+++ b/solution.py
@@ -154,9 +154,9 @@
     inputs[...] = jnp.dot(
         select, received[:, :part_width], preferred_element_type=jnp.float32
     ).astype(jnp.bfloat16)
-    for index in range(2):
-        for j in range(held_halves):
-            window = slice(j * slots, (j + 1) * slots)
+    for j in range(held_halves):
+        window = slice(j * slots, (j + 1) * slots)
+        for index in range(2):
             if index == 0:
                 held_weight = w_gate[j]
             else:
@@ -165,8 +165,8 @@
             value = jnp.dot(inputs[window, :], held_weight, preferred_element_type=jnp.float32)
             part[index, window, :] = value
             to_send[index, window, :] = value.astype(jnp.bfloat16)
-            if index == 1 and j + depth < held_halves:
-                copies[j + depth].start()
+        if j + depth < held_halves:
+            copies[j + depth].start()
 
 
 def down_kernel(slots, part, other, unit_scales, spread, w_down, out, lines):

time: 51.9 us -> 49 us (0.944)
  Pallas kernels: 18.4 us -> 15.5 us
    pallas_call x1, Pallas kernels: 12.7 us -> 9.8 us  [body(): pl.pallas_call(functools.partial(gate_up_kernel, tp_count, top_count, slo...]
where the time goes in v4:
time: 49 us; the launch traced here: 48.8 us
  blocking collectives  30.5 us (62%)
  Pallas kernels  15.5 us (32%)
  waiting for transfers between devices  1.61 us (3%)
  other arithmetic  0.73 us (1%)
    all_to_all x1, blocking collectives, body(): lax.all_to_all(outgoing, ('ep', 'tp'), split_axis=0, concat_axis=0, tiled...  17.7 us
    all_to_all x1, blocking collectives, body(): lax.all_to_all(combined.reshape(peers, own_rows, part_width), ('ep', 'tp'...  12.7 us
    pallas_call x1, Pallas kernels, body(): pl.pallas_call(functools.partial(gate_up_kernel, tp_count, top_count, slo...  9.8 us
    pallas_call x1, Pallas kernels, body(): pl.pallas_call(functools.partial(down_kernel, slots), out_shape=jax.Shape...  3.57 us
    pallas_call x1, Pallas kernels, body(): pl.pallas_call(functools.partial(prelude_kernel, held_halves, experts, ep...  2.16 us
    ppermute x1, waiting for transfers between devices, body(): other = lax.ppermute(to_send, 'tp', [(i, i ^ 1) for i in range(tp_count)])  1.61 us
  transfers between devices with their start and end apart: 1, of which 1 were waited for; matrix products, arithmetic and copies ran while one was open for 0% of the time, Pallas kernels for 0%

profile of v4, /device:TPU:0, one launch (start us, length us, event | category | flops | bytes accessed | tf_op | source)
XLA Modules:
  0.0 48.8 jit_solution(6793411967587556076)
XLA Ops:
  0.0 0.0 copy-start
  0.0 0.0 slice-start
  0.0 0.0 slice-start.1
  0.0 0.0 slice-start.2
  0.0 0.0 slice-start.3
  0.0 0.0 slice-start.4
  0.0 2.2 %prelude.1 = bf16[16,4,2176]{2,1,0:T(4,128)(2,1)S(1)} custom-call(bf16[4,4096]{1,0:T(4,128)(2,1)} %refs_0_.1, f32[1,4096]{1,0:T(1,128)} %bitcast.8, f32[64,64]{1,0:T(8,128)} %refs_2_.1, f32[64,64]{1,0:T(8,128)} %refs_3_.1, s32[8,8]{1,0:T(8,128)} %refs_4_.1, f32[8,8]{1,0:T(8,128)} %refs_5_.1), custom_call_target="tpu_custom_call" | custom-call | flops 68719476736 | bytes 1048576 | tf_op jit(solution)/shard_map/prelude/pallas_call | solution.py:218
  2.2 0.0 slice-start.5
  2.2 17.7 %all_to_all.10.received_ref = bf16[16,4,2176]{2,1,0:T(4,128)(2,1)S(1)} all-to-all(bf16[16,4,2176]{2,1,0:T(4,128)(2,1)S(1)} %prelude.1), channel_id=1, replica_groups=mesh['groups'=2,'ep'=8,'tp'=2] {'ep','tp'}, dimensions={0} | all-to-all | bytes 557056 | tf_op jit(solution)/shard_map/all_to_all | solution.py:229
  19.9 0.0 copy-done
  20.0 9.8 %gate_up.1 = (f32[2,256,384]{2,1,0:T(8,128)S(1)}, bf16[2,256,384]{2,1,0:T(8,128)(2,1)S(1)}, bf16[256,64]{1,0:T(8,128)(2,1)S(1)}) custom-call(bf16[16,4,2176]{2,1,0:T(4,128)(2,1)S(1)} %all_to_all.10.received_ref, bf16[16,2048,384]{2,1,0:T(8,128)(2,1)S(1)} %copy-done, bf16[16,2048,384]{2,1,0:T(8,128)(2,1)} %w_up.1), custom_call_target="tpu_custom_call" | custom-call | tf_op jit(solution)/shard_map/gate_up/pallas_call | solution.py:230
  29.8 0.2 collective-permute-start
  29.9 1.6 %collective-permute-done.other = bf16[2,256,384]{2,1,0:T(8,128)(2,1)S(1)} collective-permute-done((bf16[2,256,384]{2,1,0:T(8,128)(2,1)S(1)}, bf16[2,256,384]{2,1,0:T(8,128)(2,1)S(1)}, u32[]{:S(2)}, u32[]{:S(2)}) %collective-permute-start) | collective-permute-done | bytes 393248 | tf_op jit(solution)/shard_map/ppermute | solution.py:251
  31.6 0.0 slice-done
  31.6 0.0 slice-done.1
  31.6 0.0 slice-done.2
  31.6 0.0 slice-done.3
  31.6 0.0 slice-done.4
  31.6 0.0 slice-done.5
  31.6 0.0 copy-done.1
  31.6 3.6 %down.1 = bf16[64,2048]{1,0:T(8,128)(2,1)S(1)} custom-call(f32[2,256,384]{2,1,0:T(8,128)S(1)} %get-tuple-element.8.part, bf16[2,256,384]{2,1,0:T(8,128)(2,1)S(1)} %collective-permute-done.other, f32[16,2,384]{2,1,0:T(2,128)S(1)} %copy-done.1, bf16[256,64]{1,0:T(8,128)(2,1)S(1)} %get-tuple-element.10.spread, bf16[16,384,2048]{2,1,0:T(8,128)(2,1)S(1)} %bitcast.6), custom_call_target="tpu_custom_call" | custom-call | tf_op jit(solution)/shard_map/down/pallas_call | solution.py:252
  35.2 0.1 reshape.8
  35.3 12.7 %all_to_all.11 = bf16[16,4,2048]{2,1,0:T(4,128)(2,1)S(1)} all-to-all(bf16[16,4,2048]{2,1,0:T(4,128)(2,1)S(1)} %reshape.8), channel_id=1, replica_groups=mesh['groups'=2,'ep'=8,'tp'=2] {'ep','tp'}, dimensions={0} | all-to-all | bytes 524288 | tf_op jit(solution)/shard_map/all_to_all | solution.py:261
  48.0 0.7 %reduce = bf16[2,4,2048]{2,1,0:T(4,128)(2,1)} reduce(bf16[8,2,4,2048]{3,2,1,0:T(4,128)(2,1)S(1)} %bitcast.7, bf16[]{:T(256)} %constant.5), dimensions={0}, to_apply=%region_0.0.clone | reduce | flops 114688 | bytes 294914 | tf_op jit(solution)/shard_map/reduce_sum | solution.py:269
  (2 shorter events, 0.0 us)
Async XLA Ops:
  0.0 19.9 %copy-start = (bf16[16,2048,384]{2,1,0:T(8,128)(2,1)S(1)}, bf16[16,2048,384]{2,1,0:T(8,128)(2,1)}, u32[]{:S(2)}) copy-start(bf16[16,2048,384]{2,1,0:T(8,128)(2,1)} %w_gate.1) | copy-start | bytes 75497472
  0.0 31.6 %slice-start = ((s8[25165824]{0:T(1024)(128)(4,1)}), s8[4194304]{0:T(1024)(128)(4,1)S(1)}, s32[]{:S(2)}) async-start(s8[25165824]{0:T(1024)(128)(4,1)} %bitcast.5), calls=%async_computation.2 | async-start | bytes 8388608
  0.0 31.6 %slice-start.1 = ((s8[25165824]{0:T(1024)(128)(4,1)}), s8[4194304]{0:T(1024)(128)(4,1)S(1)}, s32[]{:S(2)}) async-start(s8[25165824]{0:T(1024)(128)(4,1)} %bitcast.5), calls=%async_computation.3 | async-start | bytes 8388608
  0.0 31.6 %slice-start.2 = ((s8[25165824]{0:T(1024)(128)(4,1)}), s8[4194304]{0:T(1024)(128)(4,1)S(1)}, s32[]{:S(2)}) async-start(s8[25165824]{0:T(1024)(128)(4,1)} %bitcast.5), calls=%async_computation.4 | async-start | bytes 8388608
  0.0 31.6 %slice-start.3 = ((s8[25165824]{0:T(1024)(128)(4,1)}), s8[4194304]{0:T(1024)(128)(4,1)S(1)}, s32[]{:S(2)}) async-start(s8[25165824]{0:T(1024)(128)(4,1)} %bitcast.5), calls=%async_computation.5 | async-start | bytes 8388608
  0.0 31.6 %slice-start.4 = ((s8[25165824]{0:T(1024)(128)(4,1)}), s8[4194304]{0:T(1024)(128)(4,1)S(1)}, s32[]{:S(2)}) async-start(s8[25165824]{0:T(1024)(128)(4,1)} %bitcast.5), calls=%async_computation.6 | async-start | bytes 8388608
  2.2 29.4 %slice-start.5 = ((s8[25165824]{0:T(1024)(128)(4,1)}), s8[4194304]{0:T(1024)(128)(4,1)S(1)}, s32[]{:S(2)}) async-start(s8[25165824]{0:T(1024)(128)(4,1)} %bitcast.5), calls=%async_computation.7 | async-start | bytes 8388608
  19.9 11.6 %copy-start.1 = (f32[16,2,384]{2,1,0:T(2,128)S(1)}, f32[16,2,384]{2,1,0:T(2,128)}, u32[]{:S(2)}) copy-start(f32[16,2,384]{2,1,0:T(2,128)} %unit_scales.1) | copy-start | bytes 147460
  29.8 1.8 %collective-permute-start = (bf16[2,256,384]{2,1,0:T(8,128)(2,1)S(1)}, bf16[2,256,384]{2,1,0:T(8,128)(2,1)S(1)}, u32[]{:S(2)}, u32[]{:S(2)}) collective-permute-start(bf16[2,256,384]{2,1,0:T(8,128)(2,1)S(1)} %get-tuple-element.9), channel_id=1, source_target_pairs={{0,1},{1,0},{2,3},{3,2},{4,5},{5,4},{6,7},{7,6},{8,9},{9,8},{10,11... | collective-permute-start | bytes 1179656 | tf_op jit(solution)/shard_map/ppermute | solution.py:251

commit v5 on v2

--- a/solution.py
+++ b/solution.py
@@ -10,6 +10,7 @@
 LANES = 128
 META = 128
 MIB = 1 << 20
+DOWN_SHARES = (5, 6, 1)
 
 
 def exact_dot(left, right):
@@ -103,10 +104,23 @@
             out[e * tp_count + t, :, part_width:] = tail
 
 
-def gate_up_kernel(
-    tp_count, top_count, slots, received_ref, w_gate, w_up, part, to_send, spread, inputs
-):
+def bring(w_down, first, held, sems):
+    copies = [
+        pltpu.make_async_copy(w_down.at[first + i], held.at[i], sems.at[i])
+        for i in range(held.shape[0])
+    ]
+
+    def start(i, carry):
+        pltpu.make_async_copy(w_down.at[first + i], held.at[i], sems.at[i]).start()
+        return carry
+
+    lax.fori_loop(0, len(copies), start, 0)
+    return copies
+
+
+def gate_kernel(tp_count, top_count, slots, received_ref, w_gate, w_down, part, spread, inputs, *more):
     held_halves, part_width, half_ff = w_gate.shape
+    copies = bring(w_down, 0, *more) if more else []
     peers, own_rows, _ = received_ref.shape
     all_rows = peers * own_rows
     received = received_ref[...].reshape(all_rows, part_width + META)
@@ -148,36 +162,56 @@
     ).astype(jnp.bfloat16)
     for j in range(held_halves):
         window = slice(j * slots, (j + 1) * slots)
-        rows = inputs[window, :]
-        for index, w in enumerate((w_gate, w_up)):
-            value = jnp.dot(rows, w[j], preferred_element_type=jnp.float32)
-            part[index, window, :] = value
-            to_send[index, window, :] = value.astype(jnp.bfloat16)
-
-
-def down_kernel(slots, part, other, unit_scales, spread, w_down, out, held, lines, sems):
-    held_halves = w_down.shape[0]
-    copies = [
-        pltpu.make_async_copy(w_down.at[j], held.at[j], sems.at[j]) for j in range(held_halves)
-    ]
+        part[window, :] = jnp.dot(
+            inputs[window, :], w_gate[j], preferred_element_type=jnp.float32
+        )
     for copy in copies:
-        copy.start()
-    for j in range(held_halves):
+        copy.wait()
+
+
+def up_kernel(slots, first, inputs, gate_part, w_up, w_down, part, to_send, *more):
+    copies = bring(w_down, first, *more) if more else []
+    for j in range(w_up.shape[0]):
         window = slice(j * slots, (j + 1) * slots)
-        gate = (part[0, window, :] + other[0, window, :].astype(jnp.float32)) * unit_scales[
+        value = jnp.dot(inputs[window, :], w_up[j], preferred_element_type=jnp.float32)
+        part[window, :] = value
+        to_send[0, window, :] = gate_part[window, :].astype(jnp.bfloat16)
+        to_send[1, window, :] = value.astype(jnp.bfloat16)
+    for copy in copies:
+        copy.wait()
+
+
+def bring_kernel(first, after, w_down, *more):
+    del after
+    for copy in bring(w_down, first, *more):
+        copy.wait()
+
+
+def down_kernel(slots, gate_part, up_part, other, unit_scales, spread, w_down, *more):
+    *brought, out, lines, rest, sems = more
+    first = sum(held.shape[0] for held in brought)
+    copies = bring(w_down, first, rest, sems)
+    held = [ref.at[i] for ref in (*brought, rest) for i in range(ref.shape[0])]
+    all_units = []
+    for j in range(w_down.shape[0]):
+        window = slice(j * slots, (j + 1) * slots)
+        gate = (gate_part[window, :] + other[0, window, :].astype(jnp.float32)) * unit_scales[
             j, 0:1, :
         ]
-        up = (part[1, window, :] + other[1, window, :].astype(jnp.float32)) * unit_scales[
+        up = (up_part[window, :] + other[1, window, :].astype(jnp.float32)) * unit_scales[
             j, 1:2, :
         ]
-        units = (gate / (1.0 + jnp.exp(-gate)) * up).astype(jnp.bfloat16)
-        copies[j].wait()
-        lines[window, :] = jnp.dot(
-            units, held[j], preferred_element_type=jnp.float32
+        all_units.append((gate / (1.0 + jnp.exp(-gate)) * up).astype(jnp.bfloat16))
+    for j in range(w_down.shape[0]):
+        if j >= first:
+            copies[j - first].wait()
+        lines[j * slots : (j + 1) * slots, :] = jnp.dot(
+            all_units[j], held[j][...], preferred_element_type=jnp.float32
         ).astype(jnp.bfloat16)
-    out[...] = lax.dot_general(
+    total = lax.dot_general(
         spread[...], lines[...], (((0,), (0,)), ((), ())), preferred_element_type=jnp.float32
     ).astype(jnp.bfloat16)
+    out[...] = total.reshape(out.shape)
 
 
 def body(
@@ -215,43 +249,88 @@
         scratch_shapes=[pltpu.VMEM(array.shape, array.dtype) for array in given]
         + [pltpu.SemaphoreType.DMA((len(given),))],
         cost_estimate=pl.CostEstimate(flops=1 << 36, bytes_accessed=MIB, transcendentals=0),
-        compiler_params=pltpu.CompilerParams(vmem_limit_bytes=4 * MIB),
+        compiler_params=pltpu.CompilerParams(vmem_limit_bytes=2 * MIB),
         name="prelude",
     )(*[pltpu.with_memory_space_constraint(array, pltpu.HBM) for array in given])
     received = lax.all_to_all(outgoing, ("ep", "tp"), split_axis=0, concat_axis=0, tiled=True)
-    part, to_send, spread = pl.pallas_call(
-        functools.partial(gate_up_kernel, tp_count, top_count, slots),
-        out_shape=(
-            pltpu.VMEM((2, lines, half_ff), jnp.float32),
+    in_vmem, in_hbm = (
+        functools.partial(pltpu.with_memory_space_constraint, memory_space=space)
+        for space in (pltpu.VMEM, pltpu.HBM)
+    )
+    hbm = pl.BlockSpec(memory_space=pltpu.HBM)
+
+    def brought(count):
+        shapes = [pltpu.VMEM((count,) + w_down.shape[1:], w_down.dtype)] if count else []
+        return shapes, [pltpu.SemaphoreType.DMA((count,))] if count else []
+
+    counts = [held_halves * share // 16 for share in DOWN_SHARES]
+    shapes, sems = brought(counts[0])
+    gate_part, spread, inputs, *first_down = pl.pallas_call(
+        functools.partial(gate_kernel, tp_count, top_count, slots),
+        out_shape=[
+            pltpu.VMEM((lines, half_ff), jnp.float32),
+            pltpu.VMEM((lines, all_rows), jnp.bfloat16),
+            pltpu.VMEM((lines, part_width), jnp.bfloat16),
+        ]
+        + shapes,
+        in_specs=[vmem, vmem, hbm],
+        out_specs=[vmem] * (3 + len(shapes)),
+        scratch_shapes=sems,
+        compiler_params=pltpu.CompilerParams(vmem_limit_bytes=2 * MIB),
+        name="gate",
+    )(received, in_vmem(w_gate), in_hbm(w_down))
+    shapes, sems = brought(counts[1])
+    up_part, to_send, *next_down = pl.pallas_call(
+        functools.partial(up_kernel, slots, counts[0]),
+        out_shape=[
+            pltpu.VMEM((lines, half_ff), jnp.float32),
             pltpu.VMEM((2, lines, half_ff), jnp.bfloat16),
-            pltpu.VMEM((lines, all_rows), jnp.bfloat16),
-        ),
-        in_specs=[vmem] * 3,
-        out_specs=(vmem,) * 3,
-        scratch_shapes=[pltpu.VMEM((lines, part_width), jnp.bfloat16)],
-        compiler_params=pltpu.CompilerParams(vmem_limit_bytes=5 * MIB),
-        name="gate_up",
-    )(
-        received,
-        pltpu.with_memory_space_constraint(w_gate, pltpu.VMEM),
-        pltpu.with_memory_space_constraint(w_up, pltpu.VMEM),
-    )
+        ]
+        + shapes,
+        in_specs=[vmem, vmem, vmem, hbm],
+        out_specs=[vmem] * (2 + len(shapes)),
+        scratch_shapes=sems,
+        compiler_params=pltpu.CompilerParams(vmem_limit_bytes=2 * MIB),
+        name="up",
+    )(in_vmem(inputs), in_vmem(gate_part), in_vmem(w_up), in_hbm(w_down))
     other = lax.ppermute(to_send, "tp", [(i, i ^ 1) for i in range(tp_count)])
+    shapes, sems = brought(counts[2])
+    last_down = []
+    if shapes:
+        last_down = pl.pallas_call(
+            functools.partial(bring_kernel, counts[0] + counts[1]),
+            out_shape=shapes,
+            in_specs=[vmem, hbm],
+            out_specs=[vmem],
+            scratch_shapes=sems,
+            compiler_params=pltpu.CompilerParams(vmem_limit_bytes=MIB),
+            name="bring",
+        )(in_vmem(up_part), in_hbm(w_down))
+    brought_down = [in_vmem(array) for array in (*first_down, *next_down, *last_down)]
+    rest = held_halves - sum(counts)
     combined = pl.pallas_call(
         functools.partial(down_kernel, slots),
-        out_shape=jax.ShapeDtypeStruct((all_rows, part_width), jnp.bfloat16),
-        in_specs=[vmem] * 4 + [pl.BlockSpec(memory_space=pltpu.HBM)],
+        out_shape=jax.ShapeDtypeStruct((peers, own_rows, part_width), jnp.bfloat16),
+        in_specs=[vmem] * 5 + [hbm] + [vmem] * len(brought_down),
         out_specs=vmem,
         scratch_shapes=[
-            pltpu.VMEM(w_down.shape, w_down.dtype),
             pltpu.VMEM((lines, part_width), jnp.bfloat16),
-            pltpu.SemaphoreType.DMA((held_halves,)),
+            pltpu.VMEM((rest,) + w_down.shape[1:], w_down.dtype),
+            pltpu.SemaphoreType.DMA((rest,)),
         ],
-        compiler_params=pltpu.CompilerParams(vmem_limit_bytes=36 * MIB),
+        compiler_params=pltpu.CompilerParams(vmem_limit_bytes=(2 + 3 * (rest + 1) // 2) * MIB),
         name="down",
-    )(part, other, unit_scales, spread, w_down)
+    )(
+        in_vmem(gate_part),
+        in_vmem(up_part),
+        other,
+        unit_scales,
+        in_vmem(spread),
+        in_hbm(w_down),
+        *brought_down,
+    )
     returned = lax.all_to_all(
-        combined.reshape(peers, own_rows, part_width),
+        combined,
         ("ep", "tp"),
         split_axis=0,
         concat_axis=0,

time: 52.6 us -> 47.5 us (0.903)
  Pallas kernels: 19.1 us -> 15.4 us
  waiting for transfers between devices: 1.62 us -> 0.19 us
    pallas_call x1, Pallas kernels: 8.86 us -> 4.12 us  [body(): pl.pallas_call(functools.partial(down_kernel, slots), out_shape=jax.Shape...]
    ppermute x1, waiting for transfers between devices: 1.62 us -> 0.19 us  [body(): other = lax.ppermute(to_send, 'tp', [(i, i ^ 1) for i in range(tp_count)])]
    pallas_call x1 -> x3, Pallas kernels: 8.12 us -> 9.17 us  [the longest x1 3.96 us: body(): pl.pallas_call(functools.partial(gate_kernel, tp_count, top_count, slots)...]
  transfers between devices with their start and end apart: 1 -> 1, of which waited for: 1 -> 1; matrix products, arithmetic and copies ran while one was open for 0% -> 0% of each run, Pallas kernels for 0% -> 3%
where the time goes in v5:
time: 47.5 us; the launch traced here: 47.2 us
  blocking collectives  30.5 us (64%)
  Pallas kernels  15.4 us (32%)
  other arithmetic  0.73 us (2%)
    all_to_all x1, blocking collectives, body(): lax.all_to_all(outgoing, ('ep', 'tp'), split_axis=0, concat_axis=0, tiled...  17.7 us
    all_to_all x1, blocking collectives, body(): lax.all_to_all(combined, ('ep', 'tp'), split_axis=0, concat_axis=0, tiled...  12.8 us
    pallas_call x1, Pallas kernels, body(): pl.pallas_call(functools.partial(down_kernel, slots), out_shape=jax.Shape...  4.12 us
    pallas_call x1, Pallas kernels, body(): pl.pallas_call(functools.partial(gate_kernel, tp_count, top_count, slots)...  3.96 us
    pallas_call x1, Pallas kernels, body(): pl.pallas_call(functools.partial(up_kernel, slots, counts[0]), out_shape=...  3.8 us
    pallas_call x1, Pallas kernels, body(): pl.pallas_call(functools.partial(prelude_kernel, held_halves, experts, ep...  2.16 us
    pallas_call x1, Pallas kernels, body(): pl.pallas_call(functools.partial(bring_kernel, counts[0] + counts[1]), ou...  1.42 us
  transfers between devices with their start and end apart: 1, of which 1 were waited for; matrix products, arithmetic and copies ran while one was open for 0% of the time, Pallas kernels for 3%

profile of v5, /device:TPU:0, one launch (start us, length us, event | category | flops | bytes accessed | tf_op | source)
XLA Modules:
  0.0 47.2 jit_solution(18300477878294543977)
XLA Ops:
  0.0 0.0 copy-start
  0.0 0.0 slice-start
  0.0 0.0 slice-start.1
  0.0 0.0 slice-start.4
  0.0 2.2 %prelude.1 = bf16[16,4,2176]{2,1,0:T(4,128)(2,1)S(1)} custom-call(bf16[4,4096]{1,0:T(4,128)(2,1)} %refs_0_.1, f32[1,4096]{1,0:T(1,128)} %bitcast.8, f32[64,64]{1,0:T(8,128)} %refs_2_.1, f32[64,64]{1,0:T(8,128)} %refs_3_.1, s32[8,8]{1,0:T(8,128)} %refs_4_.1, f32[8,8]{1,0:T(8,128)} %refs_5_.1), custom_call_target="tpu_custom_call" | custom-call | flops 68719476736 | bytes 1048576 | tf_op jit(solution)/shard_map/prelude/pallas_call | solution.py:244
  2.2 0.0 slice-start.5
  2.2 17.7 %all_to_all.10.received_ref = bf16[16,4,2176]{2,1,0:T(4,128)(2,1)S(1)} all-to-all(bf16[16,4,2176]{2,1,0:T(4,128)(2,1)S(1)} %prelude.1), channel_id=1, replica_groups=mesh['groups'=2,'ep'=8,'tp'=2] {'ep','tp'}, dimensions={0} | all-to-all | bytes 557056 | tf_op jit(solution)/shard_map/all_to_all | solution.py:255
  19.9 0.0 copy-done
  19.9 4.0 %gate.1 = (f32[256,384]{1,0:T(8,128)S(1)}, bf16[256,64]{1,0:T(8,128)(2,1)S(1)}, bf16[256,2048]{1,0:T(8,128)(2,1)S(1)}, bf16[5,384,2048]{2,1,0:T(8,128)(2,1)S(1)}) custom-call(bf16[16,4,2176]{2,1,0:T(4,128)(2,1)S(1)} %all_to_all.10.received_ref, bf16[16,2048,384]{2,1,0:T(8,128)(2,1)S(1)} %copy-done, bf16[16,384,2048]{2,1,0:T(8,128)(2,1)} %w_down.7), custom_call_target="tpu_custom_call" | custom-call | tf_op jit(solution)/shard_map/gate/pallas_call | solution.py:268
  23.9 0.0 slice-done
  23.9 0.0 slice-done.1
  23.9 0.0 slice-done.2
  23.9 0.0 slice-done.3
  24.0 0.0 slice-done.4
  24.0 0.0 slice-done.5
  24.0 3.8 %up.1 = (f32[256,384]{1,0:T(8,128)S(1)}, bf16[2,256,384]{2,1,0:T(8,128)(2,1)S(1)}, bf16[6,384,2048]{2,1,0:T(8,128)(2,1)S(1)}) custom-call(bf16[256,2048]{1,0:T(8,128)(2,1)S(1)} %get-tuple-element.13.inputs, f32[256,384]{1,0:T(8,128)S(1)} %get-tuple-element.12.gate_part, bf16[16,2048,384]{2,1,0:T(8,128)(2,1)S(1)} %bitcast.6, bf16[16,384,2048]{2,1,0:T(8,128)(2,1)} %w_down.7), custom_call_target="tpu_custom_call" | custom-call | tf_op jit(solution)/shard_map/up/pallas_call | solution.py:283
  27.8 0.0 copy-start.1
  27.8 0.2 collective-permute-start
  28.0 1.4 %bring.1.more_2_ = bf16[1,384,2048]{2,1,0:T(8,128)(2,1)S(1)} custom-call(f32[256,384]{1,0:T(8,128)S(1)} %get-tuple-element.14.after.up_part, bf16[16,384,2048]{2,1,0:T(8,128)(2,1)} %w_down.7), custom_call_target="tpu_custom_call" | custom-call | tf_op jit(solution)/shard_map/bring/pallas_call | solution.py:300
  29.4 0.2 collective-permute-done.other
  29.6 0.0 copy-done.1
  29.6 4.1 %down.1 = bf16[16,4,2048]{2,1,0:T(4,128)(2,1)S(1)} custom-call(f32[256,384]{1,0:T(8,128)S(1)} %get-tuple-element.12.gate_part, f32[256,384]{1,0:T(8,128)S(1)} %get-tuple-element.14.after.up_part, bf16[2,256,384]{2,1,0:T(8,128)(2,1)S(1)} %collective-permute-done.other, f32[16,2,384]{2,1,0:T(2,128)S(1)} %copy-done.1, ...), custom_call_target="tpu_custom_call" | custom-call | tf_op jit(solution)/shard_map/down/pallas_call | solution.py:311
  33.7 12.8 %all_to_all.11 = bf16[16,4,2048]{2,1,0:T(4,128)(2,1)S(1)} all-to-all(bf16[16,4,2048]{2,1,0:T(4,128)(2,1)S(1)} %down.1), channel_id=1, replica_groups=mesh['groups'=2,'ep'=8,'tp'=2] {'ep','tp'}, dimensions={0} | all-to-all | bytes 524288 | tf_op jit(solution)/shard_map/all_to_all | solution.py:332
  46.5 0.7 %reduce = bf16[2,4,2048]{2,1,0:T(4,128)(2,1)} reduce(bf16[8,2,4,2048]{3,2,1,0:T(4,128)(2,1)S(1)} %bitcast.7, bf16[]{:T(256)} %constant.5), dimensions={0}, to_apply=%region_0.0.clone | reduce | flops 114688 | bytes 294914 | tf_op jit(solution)/shard_map/reduce_sum | solution.py:340
  (3 shorter events, 0.0 us)
Async XLA Ops:
  0.0 19.9 %copy-start = (bf16[16,2048,384]{2,1,0:T(8,128)(2,1)S(1)}, bf16[16,2048,384]{2,1,0:T(8,128)(2,1)}, u32[]{:S(2)}) copy-start(bf16[16,2048,384]{2,1,0:T(8,128)(2,1)} %w_gate.1) | copy-start | bytes 75497472
  0.0 23.9 %slice-start = ((s8[25165824]{0:T(1024)(128)(4,1)}), s8[4194304]{0:T(1024)(128)(4,1)S(1)}, s32[]{:S(2)}) async-start(s8[25165824]{0:T(1024)(128)(4,1)} %bitcast.5), calls=%async_computation.2 | async-start | bytes 8388608
  0.0 23.9 %slice-start.1 = ((s8[25165824]{0:T(1024)(128)(4,1)}), s8[4194304]{0:T(1024)(128)(4,1)S(1)}, s32[]{:S(2)}) async-start(s8[25165824]{0:T(1024)(128)(4,1)} %bitcast.5), calls=%async_computation.3 | async-start | bytes 8388608
  0.0 23.9 %slice-start.2 = ((s8[25165824]{0:T(1024)(128)(4,1)}), s8[4194304]{0:T(1024)(128)(4,1)S(1)}, s32[]{:S(2)}) async-start(s8[25165824]{0:T(1024)(128)(4,1)} %bitcast.5), calls=%async_computation.4 | async-start | bytes 8388608
  0.0 23.9 %slice-start.3 = ((s8[25165824]{0:T(1024)(128)(4,1)}), s8[4194304]{0:T(1024)(128)(4,1)S(1)}, s32[]{:S(2)}) async-start(s8[25165824]{0:T(1024)(128)(4,1)} %bitcast.5), calls=%async_computation.5 | async-start | bytes 8388608
  0.0 23.9 %slice-start.4 = ((s8[25165824]{0:T(1024)(128)(4,1)}), s8[4194304]{0:T(1024)(128)(4,1)S(1)}, s32[]{:S(2)}) async-start(s8[25165824]{0:T(1024)(128)(4,1)} %bitcast.5), calls=%async_computation.6 | async-start | bytes 8388608
  2.2 21.8 %slice-start.5 = ((s8[25165824]{0:T(1024)(128)(4,1)}), s8[4194304]{0:T(1024)(128)(4,1)S(1)}, s32[]{:S(2)}) async-start(s8[25165824]{0:T(1024)(128)(4,1)} %bitcast.5), calls=%async_computation.7 | async-start | bytes 8388608
  27.8 1.8 %copy-start.1 = (f32[16,2,384]{2,1,0:T(2,128)S(1)}, f32[16,2,384]{2,1,0:T(2,128)}, u32[]{:S(2)}) copy-start(f32[16,2,384]{2,1,0:T(2,128)} %unit_scales.1) | copy-start | bytes 147460
  27.8 1.8 %collective-permute-start = (bf16[2,256,384]{2,1,0:T(8,128)(2,1)S(1)}, bf16[2,256,384]{2,1,0:T(8,128)(2,1)S(1)}, u32[]{:S(2)}, u32[]{:S(2)}) collective-permute-start(bf16[2,256,384]{2,1,0:T(8,128)(2,1)S(1)} %get-tuple-element.15), channel_id=1, source_target_pairs={{0,1},{1,0},{2,3},{3,2},{4,5},{5,4},{6,7},{7,6},{8,9},{9,8},{10,11... | collective-permute-start | bytes 1179656 | tf_op jit(solution)/shard_map/ppermute | solution.py:296

commit v6 on v5

--- a/solution.py
+++ b/solution.py
@@ -13,9 +13,14 @@
 DOWN_SHARES = (5, 6, 1)
 
 
-def exact_dot(left, right):
-    return jnp.dot(
-        left, right, precision=lax.Precision.HIGHEST, preferred_element_type=jnp.float32
+def terms(value):
+    high = value.astype(jnp.bfloat16)
+    return high, (value - high.astype(jnp.float32)).astype(jnp.bfloat16)
+
+
+def dot(left, right, contract=0):
+    return lax.dot_general(
+        left, right, (((1,), (contract,)), ((), ())), preferred_element_type=jnp.float32
     )
 
 
@@ -38,42 +43,39 @@
     lines = jnp.concatenate(
         [normed[:, t * LANES : (t + 1) * LANES] for t in range(tiles)], axis=0
     )
-    right = rot_right[...]
-    two = jnp.concatenate([right] * pack, axis=0)
+    two = jnp.concatenate([rot_right[...]] * pack, axis=0)
     two = jnp.concatenate([two] * pack, axis=1)
     square = (LANES, LANES)
     line = lax.broadcasted_iota(jnp.int32, square, 0)
     lane = lax.broadcasted_iota(jnp.int32, square, 1)
-    two = jnp.where(line // factor == lane // factor, two, 0.0)
-    lines = lax.dot_general(
-        lines,
-        two,
-        (((1,), (1,)), ((), ())),
-        precision=lax.Precision.HIGHEST,
-        preferred_element_type=jnp.float32,
-    )
+    two_high, two_low = terms(jnp.where(line // factor == lane // factor, two, 0.0))
     count = tiles * own_rows
     tall = (count, factor)
     tile_of = lax.broadcasted_iota(jnp.int32, tall, 0) // own_rows
     column = lax.broadcasted_iota(jnp.int32, tall, 1)
-    picks = [jnp.where(column == pack * tile_of + p, 1.0, 0.0) for p in range(pack)]
+    picks = [
+        jnp.where(column == pack * tile_of + p, 1.0, 0.0).astype(jnp.bfloat16)
+        for p in range(pack)
+    ]
     same_row = (
-        lax.broadcasted_iota(jnp.int32, (count, count), 0) % own_rows
-        == lax.broadcasted_iota(jnp.int32, (count, count), 1) % own_rows
-    )
-    chosen = exact_dot(jnp.concatenate(picks, axis=0), rot_left[...])
+        lax.broadcasted_iota(jnp.int32, (pack * count, count), 0) % own_rows
+        == lax.broadcasted_iota(jnp.int32, (pack * count, count), 1) % own_rows
+    )
+    rows_of = jnp.concatenate(picks, axis=0)
+    chosen = [dot(rows_of, term).astype(jnp.bfloat16) for term in terms(rot_left[...])]
+    blocks = [
+        [jnp.where(same_row, dot(term, picks[p], 1), 0.0).astype(jnp.bfloat16) for term in chosen]
+        for p in range(pack)
+    ]
+    high, low = terms(lines)
+    lines = dot(high, two_high, 1) + (dot(high, two_low, 1) + dot(low, two_high, 1))
+    high, low = terms(lines)
     turned = jnp.zeros((count, LANES), jnp.float32)
     for p_in in range(pack):
-        wide = lax.dot_general(
-            chosen,
-            picks[p_in],
-            (((1,), (1,)), ((), ())),
-            precision=lax.Precision.HIGHEST,
-            preferred_element_type=jnp.float32,
-        )
+        block_high, block_low = blocks[p_in]
+        values = dot(block_high, high) + (dot(block_high, low) + dot(block_low, high))
         for p_out in range(pack):
-            block = jnp.where(same_row, wide[p_out * count : (p_out + 1) * count, :], 0.0)
-            value = exact_dot(block, lines)
+            value = values[p_out * count : (p_out + 1) * count, :]
             shift = ((p_out - p_in) * factor) % LANES
             if shift:
                 value = pltpu.roll(value, shift, 1)
@@ -203,8 +205,9 @@
         ]
         all_units.append((gate / (1.0 + jnp.exp(-gate)) * up).astype(jnp.bfloat16))
     for j in range(w_down.shape[0]):
-        if j >= first:
-            copies[j - first].wait()
+        if j == first:
+            for copy in copies:
+                copy.wait()
         lines[j * slots : (j + 1) * slots, :] = jnp.dot(
             all_units[j], held[j][...], preferred_element_type=jnp.float32
         ).astype(jnp.bfloat16)
@@ -212,6 +215,16 @@
         spread[...], lines[...], (((0,), (0,)), ((), ())), preferred_element_type=jnp.float32
     ).astype(jnp.bfloat16)
     out[...] = total.reshape(out.shape)
+
+
+def finish_kernel(ep_count, returned, out):
+    tp_count = returned.shape[0] // ep_count
+    part_width = returned.shape[2]
+    for t in range(tp_count):
+        total = returned[t].astype(jnp.float32)
+        for e in range(1, ep_count):
+            total = total + returned[e * tp_count + t].astype(jnp.float32)
+        out[:, t * part_width : (t + 1) * part_width] = total.astype(jnp.bfloat16)
 
 
 def body(
@@ -336,9 +349,14 @@
         concat_axis=0,
         tiled=True,
     )
-    returned = returned.reshape(ep_count, tp_count, own_rows, part_width)
-    total = jnp.sum(returned.astype(jnp.float32), axis=0)
-    return total.transpose(1, 0, 2).reshape(own_rows, width).astype(jnp.bfloat16)
+    return pl.pallas_call(
+        functools.partial(finish_kernel, ep_count),
+        out_shape=jax.ShapeDtypeStruct((own_rows, width), jnp.bfloat16),
+        in_specs=[vmem],
+        out_specs=vmem,
+        compiler_params=pltpu.CompilerParams(vmem_limit_bytes=16 * MIB),
+        name="finish",
+    )(returned)
 
 
 def solution(mesh):

time: 47.5 us -> 46.8 us (0.985)
  other arithmetic: 0.73 us -> 0.01 us
    reduce_sum x1 -> x0, other arithmetic: 0.73 us -> none  [body(): total = jnp.sum(returned.astype(jnp.float32), axis=0)]
    pallas_call x0 -> x1, Pallas kernels: none -> 0.66 us  [body(): pl.pallas_call(functools.partial(finish_kernel, ep_count), out_shape=jax....]
where the time goes in v6:
time: 46.8 us; the launch traced here: 46.6 us
  blocking collectives  30.5 us (65%)
  Pallas kernels  15.5 us (33%)
    all_to_all x1, blocking collectives, body(): lax.all_to_all(outgoing, ('ep', 'tp'), split_axis=0, concat_axis=0, tiled...  17.7 us
    all_to_all x1, blocking collectives, body(): lax.all_to_all(combined, ('ep', 'tp'), split_axis=0, concat_axis=0, tiled...  12.8 us
    pallas_call x1, Pallas kernels, body(): pl.pallas_call(functools.partial(down_kernel, slots), out_shape=jax.Shape...  3.99 us
    pallas_call x1, Pallas kernels, body(): pl.pallas_call(functools.partial(gate_kernel, tp_count, top_count, slots)...  3.95 us
    pallas_call x1, Pallas kernels, body(): pl.pallas_call(functools.partial(up_kernel, slots, counts[0]), out_shape=...  3.8 us
    pallas_call x1, Pallas kernels, body(): pl.pallas_call(functools.partial(prelude_kernel, held_halves, experts, ep...  1.71 us
    pallas_call x1, Pallas kernels, body(): pl.pallas_call(functools.partial(bring_kernel, counts[0] + counts[1]), ou...  1.42 us
  transfers between devices with their start and end apart: 1, of which 1 were waited for; matrix products, arithmetic and copies ran while one was open for 0% of the time, Pallas kernels for 3%

profile of v6, /device:TPU:0, one launch (start us, length us, event | category | flops | bytes accessed | tf_op | source)
XLA Modules:
  0.0 46.6 jit_solution(14061409887052655915)
XLA Ops:
  0.0 0.0 copy-start
  0.0 0.0 slice-start
  0.0 0.0 slice-start.1
  0.0 0.0 slice-start.4
  0.0 1.7 %prelude.1 = bf16[16,4,2176]{2,1,0:T(4,128)(2,1)S(1)} custom-call(bf16[4,4096]{1,0:T(4,128)(2,1)} %refs_0_.1, f32[1,4096]{1,0:T(1,128)} %bitcast.3, f32[64,64]{1,0:T(8,128)} %refs_2_.1, f32[64,64]{1,0:T(8,128)} %refs_3_.1, s32[8,8]{1,0:T(8,128)} %refs_4_.1, f32[8,8]{1,0:T(8,128)} %refs_5_.1), custom_call_target="tpu_custom_call" | custom-call | flops 68719476736 | bytes 1048576 | tf_op jit(solution)/shard_map/prelude/pallas_call | solution.py:257
  1.7 0.0 slice-start.5
  1.8 17.7 %all_to_all.10.received_ref = bf16[16,4,2176]{2,1,0:T(4,128)(2,1)S(1)} all-to-all(bf16[16,4,2176]{2,1,0:T(4,128)(2,1)S(1)} %prelude.1), channel_id=1, replica_groups=mesh['groups'=2,'ep'=8,'tp'=2] {'ep','tp'}, dimensions={0} | all-to-all | bytes 557056 | tf_op jit(solution)/shard_map/all_to_all | solution.py:268
  19.5 0.0 copy-done
  19.5 4.0 %gate.1 = (f32[256,384]{1,0:T(8,128)S(1)}, bf16[256,64]{1,0:T(8,128)(2,1)S(1)}, bf16[256,2048]{1,0:T(8,128)(2,1)S(1)}, bf16[5,384,2048]{2,1,0:T(8,128)(2,1)S(1)}) custom-call(bf16[16,4,2176]{2,1,0:T(4,128)(2,1)S(1)} %all_to_all.10.received_ref, bf16[16,2048,384]{2,1,0:T(8,128)(2,1)S(1)} %copy-done, bf16[16,384,2048]{2,1,0:T(8,128)(2,1)} %w_down.7), custom_call_target="tpu_custom_call" | custom-call | tf_op jit(solution)/shard_map/gate/pallas_call | solution.py:281
  23.5 0.0 slice-done
  23.5 0.0 slice-done.1
  23.5 0.0 slice-done.2
  23.5 0.0 slice-done.3
  23.5 0.0 slice-done.4
  23.5 0.0 slice-done.5
  23.5 3.8 %up.1 = (f32[256,384]{1,0:T(8,128)S(1)}, bf16[2,256,384]{2,1,0:T(8,128)(2,1)S(1)}, bf16[6,384,2048]{2,1,0:T(8,128)(2,1)S(1)}) custom-call(bf16[256,2048]{1,0:T(8,128)(2,1)S(1)} %get-tuple-element.13.inputs, f32[256,384]{1,0:T(8,128)S(1)} %get-tuple-element.12.gate_part, bf16[16,2048,384]{2,1,0:T(8,128)(2,1)S(1)} %bitcast.2, bf16[16,384,2048]{2,1,0:T(8,128)(2,1)} %w_down.7), custom_call_target="tpu_custom_call" | custom-call | tf_op jit(solution)/shard_map/up/pallas_call | solution.py:296
  27.3 0.0 copy-start.1
  27.4 0.2 collective-permute-start
  27.5 1.4 %bring.1.more_2_ = bf16[1,384,2048]{2,1,0:T(8,128)(2,1)S(1)} custom-call(f32[256,384]{1,0:T(8,128)S(1)} %get-tuple-element.14.after.up_part, bf16[16,384,2048]{2,1,0:T(8,128)(2,1)} %w_down.7), custom_call_target="tpu_custom_call" | custom-call | tf_op jit(solution)/shard_map/bring/pallas_call | solution.py:313
  29.0 0.2 collective-permute-done.other
  29.1 0.0 copy-done.1
  29.1 4.0 %down.1 = bf16[16,4,2048]{2,1,0:T(4,128)(2,1)S(1)} custom-call(f32[256,384]{1,0:T(8,128)S(1)} %get-tuple-element.12.gate_part, f32[256,384]{1,0:T(8,128)S(1)} %get-tuple-element.14.after.up_part, bf16[2,256,384]{2,1,0:T(8,128)(2,1)S(1)} %collective-permute-done.other, f32[16,2,384]{2,1,0:T(2,128)S(1)} %copy-done.1, ...), custom_call_target="tpu_custom_call" | custom-call | tf_op jit(solution)/shard_map/down/pallas_call | solution.py:324
  33.1 12.8 %all_to_all.11.returned = bf16[16,4,2048]{2,1,0:T(4,128)(2,1)S(1)} all-to-all(bf16[16,4,2048]{2,1,0:T(4,128)(2,1)S(1)} %down.1), channel_id=1, replica_groups=mesh['groups'=2,'ep'=8,'tp'=2] {'ep','tp'}, dimensions={0} | all-to-all | bytes 524288 | tf_op jit(solution)/shard_map/all_to_all | solution.py:345
  45.9 0.7 %finish.1 = bf16[4,4096]{1,0:T(4,128)(2,1)} custom-call(bf16[16,4,2048]{2,1,0:T(4,128)(2,1)S(1)} %all_to_all.11.returned), custom_call_target="tpu_custom_call" | custom-call | tf_op jit(solution)/shard_map/finish/pallas_call | solution.py:352
  (3 shorter events, 0.0 us)
Async XLA Ops:
  0.0 19.5 %copy-start = (bf16[16,2048,384]{2,1,0:T(8,128)(2,1)S(1)}, bf16[16,2048,384]{2,1,0:T(8,128)(2,1)}, u32[]{:S(2)}) copy-start(bf16[16,2048,384]{2,1,0:T(8,128)(2,1)} %w_gate.1) | copy-start | bytes 75497472
  0.0 23.5 %slice-start = ((s8[25165824]{0:T(1024)(128)(4,1)}), s8[4194304]{0:T(1024)(128)(4,1)S(1)}, s32[]{:S(2)}) async-start(s8[25165824]{0:T(1024)(128)(4,1)} %bitcast.1), calls=%async_computation.2 | async-start | bytes 8388608
  0.0 23.5 %slice-start.1 = ((s8[25165824]{0:T(1024)(128)(4,1)}), s8[4194304]{0:T(1024)(128)(4,1)S(1)}, s32[]{:S(2)}) async-start(s8[25165824]{0:T(1024)(128)(4,1)} %bitcast.1), calls=%async_computation.3 | async-start | bytes 8388608
  0.0 23.5 %slice-start.2 = ((s8[25165824]{0:T(1024)(128)(4,1)}), s8[4194304]{0:T(1024)(128)(4,1)S(1)}, s32[]{:S(2)}) async-start(s8[25165824]{0:T(1024)(128)(4,1)} %bitcast.1), calls=%async_computation.4 | async-start | bytes 8388608
  0.0 23.5 %slice-start.3 = ((s8[25165824]{0:T(1024)(128)(4,1)}), s8[4194304]{0:T(1024)(128)(4,1)S(1)}, s32[]{:S(2)}) async-start(s8[25165824]{0:T(1024)(128)(4,1)} %bitcast.1), calls=%async_computation.5 | async-start | bytes 8388608
  0.0 23.5 %slice-start.4 = ((s8[25165824]{0:T(1024)(128)(4,1)}), s8[4194304]{0:T(1024)(128)(4,1)S(1)}, s32[]{:S(2)}) async-start(s8[25165824]{0:T(1024)(128)(4,1)} %bitcast.1), calls=%async_computation.6 | async-start | bytes 8388608
  1.7 21.8 %slice-start.5 = ((s8[25165824]{0:T(1024)(128)(4,1)}), s8[4194304]{0:T(1024)(128)(4,1)S(1)}, s32[]{:S(2)}) async-start(s8[25165824]{0:T(1024)(128)(4,1)} %bitcast.1), calls=%async_computation.7 | async-start | bytes 8388608
  27.3 1.8 %copy-start.1 = (f32[16,2,384]{2,1,0:T(2,128)S(1)}, f32[16,2,384]{2,1,0:T(2,128)}, u32[]{:S(2)}) copy-start(f32[16,2,384]{2,1,0:T(2,128)} %unit_scales.1) | copy-start | bytes 147460
  27.4 1.8 %collective-permute-start = (bf16[2,256,384]{2,1,0:T(8,128)(2,1)S(1)}, bf16[2,256,384]{2,1,0:T(8,128)(2,1)S(1)}, u32[]{:S(2)}, u32[]{:S(2)}) collective-permute-start(bf16[2,256,384]{2,1,0:T(8,128)(2,1)S(1)} %get-tuple-element.15), channel_id=1, source_target_pairs={{0,1},{1,0},{2,3},{3,2},{4,5},{5,4},{6,7},{7,6},{8,9},{9,8},{10,11... | collective-permute-start | bytes 1179656 | tf_op jit(solution)/shard_map/ppermute | solution.py:309

commit v7 on v6

--- a/solution.py
+++ b/solution.py
@@ -120,6 +120,10 @@
     return copies
 
 
+def pass_kernel(given, out):
+    del given, out
+
+
 def gate_kernel(tp_count, top_count, slots, received_ref, w_gate, w_down, part, spread, inputs, *more):
     held_halves, part_width, half_ff = w_gate.shape
     copies = bring(w_down, 0, *more) if more else []
@@ -153,11 +157,7 @@
     slot_index = lax.broadcasted_iota(jnp.int32, (slots, all_rows), 0).astype(jnp.float32)
     selects = []
     for j in range(held_halves):
-        select = rank[j : j + 1, :] == slot_index
-        selects.append(jnp.where(select, 1.0, 0.0))
-        spread[j * slots : (j + 1) * slots, :] = jnp.where(
-            select, weight[j : j + 1, :], 0.0
-        ).astype(jnp.bfloat16)
+        selects.append(jnp.where(rank[j : j + 1, :] == slot_index, 1.0, 0.0))
     select = jnp.concatenate(selects, axis=0).astype(jnp.bfloat16)
     inputs[...] = jnp.dot(
         select, received[:, :part_width], preferred_element_type=jnp.float32
@@ -167,6 +167,10 @@
         part[window, :] = jnp.dot(
             inputs[window, :], w_gate[j], preferred_element_type=jnp.float32
         )
+    for j in range(held_halves):
+        spread[j * slots : (j + 1) * slots, :] = jnp.where(
+            rank[j : j + 1, :] == slot_index, weight[j : j + 1, :], 0.0
+        ).astype(jnp.bfloat16)
     for copy in copies:
         copy.wait()
 
@@ -261,10 +265,19 @@
         out_specs=vmem,
         scratch_shapes=[pltpu.VMEM(array.shape, array.dtype) for array in given]
         + [pltpu.SemaphoreType.DMA((len(given),))],
-        cost_estimate=pl.CostEstimate(flops=1 << 36, bytes_accessed=MIB, transcendentals=0),
         compiler_params=pltpu.CompilerParams(vmem_limit_bytes=2 * MIB),
         name="prelude",
     )(*[pltpu.with_memory_space_constraint(array, pltpu.HBM) for array in given])
+    outgoing = pl.pallas_call(
+        pass_kernel,
+        out_shape=pltpu.VMEM(outgoing.shape, outgoing.dtype),
+        in_specs=[vmem],
+        out_specs=vmem,
+        input_output_aliases={0: 0},
+        cost_estimate=pl.CostEstimate(flops=1 << 36, bytes_accessed=MIB, transcendentals=0),
+        compiler_params=pltpu.CompilerParams(vmem_limit_bytes=MIB),
+        name="pass_on",
+    )(pltpu.with_memory_space_constraint(outgoing, pltpu.VMEM))
     received = lax.all_to_all(outgoing, ("ep", "tp"), split_axis=0, concat_axis=0, tiled=True)
     in_vmem, in_hbm = (
         functools.partial(pltpu.with_memory_space_constraint, memory_space=space)

time: 46.8 us -> 46.9 us (level)
  no operation moved by 1% of the time
where the time goes in v7:
time: 46.9 us; the launch traced here: 46.7 us
  blocking collectives  30.7 us (65%)
  Pallas kernels  15.4 us (33%)
    all_to_all x1, blocking collectives, body(): lax.all_to_all(outgoing, ('ep', 'tp'), split_axis=0, concat_axis=0, tiled...  17.7 us
    all_to_all x1, blocking collectives, body(): lax.all_to_all(combined, ('ep', 'tp'), split_axis=0, concat_axis=0, tiled...  13 us
    pallas_call x1, Pallas kernels, body(): pl.pallas_call(functools.partial(down_kernel, slots), out_shape=jax.Shape...  3.99 us
    pallas_call x1, Pallas kernels, body(): pl.pallas_call(functools.partial(gate_kernel, tp_count, top_count, slots)...  3.95 us
    pallas_call x1, Pallas kernels, body(): pl.pallas_call(functools.partial(up_kernel, slots, counts[0]), out_shape=...  3.8 us
    pallas_call x1, Pallas kernels, body(): pl.pallas_call(functools.partial(prelude_kernel, held_halves, experts, ep...  1.56 us
    pallas_call x1, Pallas kernels, body(): pl.pallas_call(functools.partial(bring_kernel, counts[0] + counts[1]), ou...  1.42 us
  transfers between devices with their start and end apart: 1, of which 1 were waited for; matrix products, arithmetic and copies ran while one was open for 0% of the time, Pallas kernels for 3%

profile of v7, /device:TPU:0, one launch (start us, length us, event | category | flops | bytes accessed | tf_op | source)
XLA Modules:
  0.0 46.7 jit_solution(1217547183699264065)
XLA Ops:
  0.0 1.6 %prelude.1.given = bf16[16,4,2176]{2,1,0:T(4,128)(2,1)S(1)} custom-call(bf16[4,4096]{1,0:T(4,128)(2,1)} %refs_0_.1, f32[1,4096]{1,0:T(1,128)} %bitcast.3, f32[64,64]{1,0:T(8,128)} %refs_2_.1, f32[64,64]{1,0:T(8,128)} %refs_3_.1, s32[8,8]{1,0:T(8,128)} %refs_4_.1, f32[8,8]{1,0:T(8,128)} %refs_5_.1), custom_call_target="tpu_custom_call" | custom-call | tf_op jit(solution)/shard_map/prelude/pallas_call | solution.py:261
  1.6 0.0 copy-start
  1.6 0.0 slice-start
  1.6 0.0 slice-start.1
  1.6 0.0 slice-start.2
  1.6 0.0 slice-start.3
  1.6 0.0 slice-start.4
  1.7 0.0 slice-start.5
  1.7 17.7 %all_to_all.10.received_ref = bf16[16,4,2176]{2,1,0:T(4,128)(2,1)S(1)} all-to-all(bf16[16,4,2176]{2,1,0:T(4,128)(2,1)S(1)} %pass_on.1), channel_id=1, replica_groups=mesh['groups'=2,'ep'=8,'tp'=2] {'ep','tp'}, dimensions={0} | all-to-all | bytes 557056 | tf_op jit(solution)/shard_map/all_to_all | solution.py:281
  19.4 0.0 copy-done
  19.4 3.9 %gate.1 = (f32[256,384]{1,0:T(8,128)S(1)}, bf16[256,64]{1,0:T(8,128)(2,1)S(1)}, bf16[256,2048]{1,0:T(8,128)(2,1)S(1)}, bf16[5,384,2048]{2,1,0:T(8,128)(2,1)S(1)}) custom-call(bf16[16,4,2176]{2,1,0:T(4,128)(2,1)S(1)} %all_to_all.10.received_ref, bf16[16,2048,384]{2,1,0:T(8,128)(2,1)S(1)} %copy-done, bf16[16,384,2048]{2,1,0:T(8,128)(2,1)} %w_down.7), custom_call_target="tpu_custom_call" | custom-call | tf_op jit(solution)/shard_map/gate/pallas_call | solution.py:294
  23.4 0.0 slice-done
  23.4 0.0 slice-done.1
  23.4 0.0 slice-done.2
  23.4 0.0 slice-done.3
  23.4 0.0 slice-done.4
  23.4 3.8 %up.1 = (f32[256,384]{1,0:T(8,128)S(1)}, bf16[2,256,384]{2,1,0:T(8,128)(2,1)S(1)}, bf16[6,384,2048]{2,1,0:T(8,128)(2,1)S(1)}) custom-call(bf16[256,2048]{1,0:T(8,128)(2,1)S(1)} %get-tuple-element.13.inputs, f32[256,384]{1,0:T(8,128)S(1)} %get-tuple-element.12.gate_part, bf16[16,2048,384]{2,1,0:T(8,128)(2,1)S(1)} %bitcast.2, bf16[16,384,2048]{2,1,0:T(8,128)(2,1)} %w_down.7), custom_call_target="tpu_custom_call" | custom-call | tf_op jit(solution)/shard_map/up/pallas_call | solution.py:309
  27.2 0.0 copy-start.1
  27.2 0.2 collective-permute-start
  27.4 1.4 %bring.1.more_2_ = bf16[1,384,2048]{2,1,0:T(8,128)(2,1)S(1)} custom-call(f32[256,384]{1,0:T(8,128)S(1)} %get-tuple-element.14.after.up_part, bf16[16,384,2048]{2,1,0:T(8,128)(2,1)} %w_down.7), custom_call_target="tpu_custom_call" | custom-call | tf_op jit(solution)/shard_map/bring/pallas_call | solution.py:326
  28.8 0.2 collective-permute-done.other
  29.0 4.0 %down.1 = bf16[16,4,2048]{2,1,0:T(4,128)(2,1)S(1)} custom-call(f32[256,384]{1,0:T(8,128)S(1)} %get-tuple-element.12.gate_part, f32[256,384]{1,0:T(8,128)S(1)} %get-tuple-element.14.after.up_part, bf16[2,256,384]{2,1,0:T(8,128)(2,1)S(1)} %collective-permute-done.other, f32[16,2,384]{2,1,0:T(2,128)S(1)} %copy-done.1, ...), custom_call_target="tpu_custom_call" | custom-call | tf_op jit(solution)/shard_map/down/pallas_call | solution.py:337
  33.0 13.0 %all_to_all.11.returned = bf16[16,4,2048]{2,1,0:T(4,128)(2,1)S(1)} all-to-all(bf16[16,4,2048]{2,1,0:T(4,128)(2,1)S(1)} %down.1), channel_id=1, replica_groups=mesh['groups'=2,'ep'=8,'tp'=2] {'ep','tp'}, dimensions={0} | all-to-all | bytes 524288 | tf_op jit(solution)/shard_map/all_to_all | solution.py:358
  46.0 0.7 %finish.1 = bf16[4,4096]{1,0:T(4,128)(2,1)} custom-call(bf16[16,4,2048]{2,1,0:T(4,128)(2,1)S(1)} %all_to_all.11.returned), custom_call_target="tpu_custom_call" | custom-call | tf_op jit(solution)/shard_map/finish/pallas_call | solution.py:365
  (4 shorter events, 0.0 us)
Async XLA Ops:
  1.6 17.8 %copy-start = (bf16[16,2048,384]{2,1,0:T(8,128)(2,1)S(1)}, bf16[16,2048,384]{2,1,0:T(8,128)(2,1)}, u32[]{:S(2)}) copy-start(bf16[16,2048,384]{2,1,0:T(8,128)(2,1)} %w_gate.1) | copy-start | bytes 75497472
  1.6 21.8 %slice-start = ((s8[25165824]{0:T(1024)(128)(4,1)}), s8[4194304]{0:T(1024)(128)(4,1)S(1)}, s32[]{:S(2)}) async-start(s8[25165824]{0:T(1024)(128)(4,1)} %bitcast.1), calls=%async_computation.2 | async-start | bytes 8388608
  1.6 21.8 %slice-start.1 = ((s8[25165824]{0:T(1024)(128)(4,1)}), s8[4194304]{0:T(1024)(128)(4,1)S(1)}, s32[]{:S(2)}) async-start(s8[25165824]{0:T(1024)(128)(4,1)} %bitcast.1), calls=%async_computation.3 | async-start | bytes 8388608
  1.6 21.8 %slice-start.2 = ((s8[25165824]{0:T(1024)(128)(4,1)}), s8[4194304]{0:T(1024)(128)(4,1)S(1)}, s32[]{:S(2)}) async-start(s8[25165824]{0:T(1024)(128)(4,1)} %bitcast.1), calls=%async_computation.4 | async-start | bytes 8388608
  1.6 21.8 %slice-start.3 = ((s8[25165824]{0:T(1024)(128)(4,1)}), s8[4194304]{0:T(1024)(128)(4,1)S(1)}, s32[]{:S(2)}) async-start(s8[25165824]{0:T(1024)(128)(4,1)} %bitcast.1), calls=%async_computation.5 | async-start | bytes 8388608
  1.6 21.8 %slice-start.4 = ((s8[25165824]{0:T(1024)(128)(4,1)}), s8[4194304]{0:T(1024)(128)(4,1)S(1)}, s32[]{:S(2)}) async-start(s8[25165824]{0:T(1024)(128)(4,1)} %bitcast.1), calls=%async_computation.6 | async-start | bytes 8388608
  1.7 21.8 %slice-start.5 = ((s8[25165824]{0:T(1024)(128)(4,1)}), s8[4194304]{0:T(1024)(128)(4,1)S(1)}, s32[]{:S(2)}) async-start(s8[25165824]{0:T(1024)(128)(4,1)} %bitcast.1), calls=%async_computation.7 | async-start | bytes 8388608
  27.2 1.8 %copy-start.1 = (f32[16,2,384]{2,1,0:T(2,128)S(1)}, f32[16,2,384]{2,1,0:T(2,128)}, u32[]{:S(2)}) copy-start(f32[16,2,384]{2,1,0:T(2,128)} %unit_scales.1) | copy-start | bytes 147460
  27.2 1.8 %collective-permute-start = (bf16[2,256,384]{2,1,0:T(8,128)(2,1)S(1)}, bf16[2,256,384]{2,1,0:T(8,128)(2,1)S(1)}, u32[]{:S(2)}, u32[]{:S(2)}) collective-permute-start(bf16[2,256,384]{2,1,0:T(8,128)(2,1)S(1)} %get-tuple-element.15), channel_id=1, source_target_pairs={{0,1},{1,0},{2,3},{3,2},{4,5},{5,4},{6,7},{7,6},{8,9},{9,8},{10,11... | collective-permute-start | bytes 1179656 | tf_op jit(solution)/shard_map/ppermute | solution.py:322

commit v8 on v6

--- a/solution.py
+++ b/solution.py
@@ -153,11 +153,7 @@
     slot_index = lax.broadcasted_iota(jnp.int32, (slots, all_rows), 0).astype(jnp.float32)
     selects = []
     for j in range(held_halves):
-        select = rank[j : j + 1, :] == slot_index
-        selects.append(jnp.where(select, 1.0, 0.0))
-        spread[j * slots : (j + 1) * slots, :] = jnp.where(
-            select, weight[j : j + 1, :], 0.0
-        ).astype(jnp.bfloat16)
+        selects.append(jnp.where(rank[j : j + 1, :] == slot_index, 1.0, 0.0))
     select = jnp.concatenate(selects, axis=0).astype(jnp.bfloat16)
     inputs[...] = jnp.dot(
         select, received[:, :part_width], preferred_element_type=jnp.float32
@@ -167,6 +163,10 @@
         part[window, :] = jnp.dot(
             inputs[window, :], w_gate[j], preferred_element_type=jnp.float32
         )
+    for j in range(held_halves):
+        spread[j * slots : (j + 1) * slots, :] = jnp.where(
+            rank[j : j + 1, :] == slot_index, weight[j : j + 1, :], 0.0
+        ).astype(jnp.bfloat16)
     for copy in copies:
         copy.wait()
 

time: 46.8 us -> 46.8 us (level)
  no operation moved by 1% of the time
where the time goes in v8:
time: 46.8 us; the launch traced here: 46.6 us
  blocking collectives  30.5 us (65%)
  Pallas kernels  15.5 us (33%)
    all_to_all x1, blocking collectives, body(): lax.all_to_all(outgoing, ('ep', 'tp'), split_axis=0, concat_axis=0, tiled...  17.7 us
    all_to_all x1, blocking collectives, body(): lax.all_to_all(combined, ('ep', 'tp'), split_axis=0, concat_axis=0, tiled...  12.8 us
    pallas_call x1, Pallas kernels, body(): pl.pallas_call(functools.partial(down_kernel, slots), out_shape=jax.Shape...  3.99 us
    pallas_call x1, Pallas kernels, body(): pl.pallas_call(functools.partial(gate_kernel, tp_count, top_count, slots)...  3.95 us
    pallas_call x1, Pallas kernels, body(): pl.pallas_call(functools.partial(up_kernel, slots, counts[0]), out_shape=...  3.8 us
    pallas_call x1, Pallas kernels, body(): pl.pallas_call(functools.partial(prelude_kernel, held_halves, experts, ep...  1.71 us
    pallas_call x1, Pallas kernels, body(): pl.pallas_call(functools.partial(bring_kernel, counts[0] + counts[1]), ou...  1.42 us
  transfers between devices with their start and end apart: 1, of which 1 were waited for; matrix products, arithmetic and copies ran while one was open for 0% of the time, Pallas kernels for 3%

profile of v8, /device:TPU:0, one launch (start us, length us, event | category | flops | bytes accessed | tf_op | source)
XLA Modules:
  0.0 46.6 jit_solution(17396765711065203739)
XLA Ops:
  0.0 0.0 copy-start
  0.0 0.0 slice-start
  0.0 0.0 slice-start.1
  0.0 0.0 slice-start.4
  0.0 1.7 %prelude.1 = bf16[16,4,2176]{2,1,0:T(4,128)(2,1)S(1)} custom-call(bf16[4,4096]{1,0:T(4,128)(2,1)} %refs_0_.1, f32[1,4096]{1,0:T(1,128)} %bitcast.3, f32[64,64]{1,0:T(8,128)} %refs_2_.1, f32[64,64]{1,0:T(8,128)} %refs_3_.1, s32[8,8]{1,0:T(8,128)} %refs_4_.1, f32[8,8]{1,0:T(8,128)} %refs_5_.1), custom_call_target="tpu_custom_call" | custom-call | flops 68719476736 | bytes 1048576 | tf_op jit(solution)/shard_map/prelude/pallas_call | solution.py:257
  1.7 0.0 slice-start.5
  1.8 17.7 %all_to_all.10.received_ref = bf16[16,4,2176]{2,1,0:T(4,128)(2,1)S(1)} all-to-all(bf16[16,4,2176]{2,1,0:T(4,128)(2,1)S(1)} %prelude.1), channel_id=1, replica_groups=mesh['groups'=2,'ep'=8,'tp'=2] {'ep','tp'}, dimensions={0} | all-to-all | bytes 557056 | tf_op jit(solution)/shard_map/all_to_all | solution.py:268
  19.5 0.0 copy-done
  19.5 4.0 %gate.1 = (f32[256,384]{1,0:T(8,128)S(1)}, bf16[256,64]{1,0:T(8,128)(2,1)S(1)}, bf16[256,2048]{1,0:T(8,128)(2,1)S(1)}, bf16[5,384,2048]{2,1,0:T(8,128)(2,1)S(1)}) custom-call(bf16[16,4,2176]{2,1,0:T(4,128)(2,1)S(1)} %all_to_all.10.received_ref, bf16[16,2048,384]{2,1,0:T(8,128)(2,1)S(1)} %copy-done, bf16[16,384,2048]{2,1,0:T(8,128)(2,1)} %w_down.7), custom_call_target="tpu_custom_call" | custom-call | tf_op jit(solution)/shard_map/gate/pallas_call | solution.py:281
  23.5 0.0 slice-done
  23.5 0.0 slice-done.1
  23.5 0.0 slice-done.2
  23.5 0.0 slice-done.3
  23.5 0.0 slice-done.4
  23.5 0.0 slice-done.5
  23.5 3.8 %up.1 = (f32[256,384]{1,0:T(8,128)S(1)}, bf16[2,256,384]{2,1,0:T(8,128)(2,1)S(1)}, bf16[6,384,2048]{2,1,0:T(8,128)(2,1)S(1)}) custom-call(bf16[256,2048]{1,0:T(8,128)(2,1)S(1)} %get-tuple-element.13.inputs, f32[256,384]{1,0:T(8,128)S(1)} %get-tuple-element.12.gate_part, bf16[16,2048,384]{2,1,0:T(8,128)(2,1)S(1)} %bitcast.2, bf16[16,384,2048]{2,1,0:T(8,128)(2,1)} %w_down.7), custom_call_target="tpu_custom_call" | custom-call | tf_op jit(solution)/shard_map/up/pallas_call | solution.py:296
  27.3 0.0 copy-start.1
  27.4 0.2 collective-permute-start
  27.5 1.4 %bring.1.more_2_ = bf16[1,384,2048]{2,1,0:T(8,128)(2,1)S(1)} custom-call(f32[256,384]{1,0:T(8,128)S(1)} %get-tuple-element.14.after.up_part, bf16[16,384,2048]{2,1,0:T(8,128)(2,1)} %w_down.7), custom_call_target="tpu_custom_call" | custom-call | tf_op jit(solution)/shard_map/bring/pallas_call | solution.py:313
  28.9 0.2 collective-permute-done.other
  29.1 0.0 copy-done.1
  29.1 4.0 %down.1 = bf16[16,4,2048]{2,1,0:T(4,128)(2,1)S(1)} custom-call(f32[256,384]{1,0:T(8,128)S(1)} %get-tuple-element.12.gate_part, f32[256,384]{1,0:T(8,128)S(1)} %get-tuple-element.14.after.up_part, bf16[2,256,384]{2,1,0:T(8,128)(2,1)S(1)} %collective-permute-done.other, f32[16,2,384]{2,1,0:T(2,128)S(1)} %copy-done.1, ...), custom_call_target="tpu_custom_call" | custom-call | tf_op jit(solution)/shard_map/down/pallas_call | solution.py:324
  33.1 12.8 %all_to_all.11.returned = bf16[16,4,2048]{2,1,0:T(4,128)(2,1)S(1)} all-to-all(bf16[16,4,2048]{2,1,0:T(4,128)(2,1)S(1)} %down.1), channel_id=1, replica_groups=mesh['groups'=2,'ep'=8,'tp'=2] {'ep','tp'}, dimensions={0} | all-to-all | bytes 524288 | tf_op jit(solution)/shard_map/all_to_all | solution.py:345
  45.9 0.7 %finish.1 = bf16[4,4096]{1,0:T(4,128)(2,1)} custom-call(bf16[16,4,2048]{2,1,0:T(4,128)(2,1)S(1)} %all_to_all.11.returned), custom_call_target="tpu_custom_call" | custom-call | tf_op jit(solution)/shard_map/finish/pallas_call | solution.py:352
  (3 shorter events, 0.0 us)
Async XLA Ops:
  0.0 19.5 %copy-start = (bf16[16,2048,384]{2,1,0:T(8,128)(2,1)S(1)}, bf16[16,2048,384]{2,1,0:T(8,128)(2,1)}, u32[]{:S(2)}) copy-start(bf16[16,2048,384]{2,1,0:T(8,128)(2,1)} %w_gate.1) | copy-start | bytes 75497472
  0.0 23.5 %slice-start = ((s8[25165824]{0:T(1024)(128)(4,1)}), s8[4194304]{0:T(1024)(128)(4,1)S(1)}, s32[]{:S(2)}) async-start(s8[25165824]{0:T(1024)(128)(4,1)} %bitcast.1), calls=%async_computation.2 | async-start | bytes 8388608
  0.0 23.5 %slice-start.1 = ((s8[25165824]{0:T(1024)(128)(4,1)}), s8[4194304]{0:T(1024)(128)(4,1)S(1)}, s32[]{:S(2)}) async-start(s8[25165824]{0:T(1024)(128)(4,1)} %bitcast.1), calls=%async_computation.3 | async-start | bytes 8388608
  0.0 23.5 %slice-start.2 = ((s8[25165824]{0:T(1024)(128)(4,1)}), s8[4194304]{0:T(1024)(128)(4,1)S(1)}, s32[]{:S(2)}) async-start(s8[25165824]{0:T(1024)(128)(4,1)} %bitcast.1), calls=%async_computation.4 | async-start | bytes 8388608
  0.0 23.5 %slice-start.3 = ((s8[25165824]{0:T(1024)(128)(4,1)}), s8[4194304]{0:T(1024)(128)(4,1)S(1)}, s32[]{:S(2)}) async-start(s8[25165824]{0:T(1024)(128)(4,1)} %bitcast.1), calls=%async_computation.5 | async-start | bytes 8388608
  0.0 23.5 %slice-start.4 = ((s8[25165824]{0:T(1024)(128)(4,1)}), s8[4194304]{0:T(1024)(128)(4,1)S(1)}, s32[]{:S(2)}) async-start(s8[25165824]{0:T(1024)(128)(4,1)} %bitcast.1), calls=%async_computation.6 | async-start | bytes 8388608
  1.7 21.8 %slice-start.5 = ((s8[25165824]{0:T(1024)(128)(4,1)}), s8[4194304]{0:T(1024)(128)(4,1)S(1)}, s32[]{:S(2)}) async-start(s8[25165824]{0:T(1024)(128)(4,1)} %bitcast.1), calls=%async_computation.7 | async-start | bytes 8388608
  27.3 1.8 %copy-start.1 = (f32[16,2,384]{2,1,0:T(2,128)S(1)}, f32[16,2,384]{2,1,0:T(2,128)}, u32[]{:S(2)}) copy-start(f32[16,2,384]{2,1,0:T(2,128)} %unit_scales.1) | copy-start | bytes 147460
  27.4 1.8 %collective-permute-start = (bf16[2,256,384]{2,1,0:T(8,128)(2,1)S(1)}, bf16[2,256,384]{2,1,0:T(8,128)(2,1)S(1)}, u32[]{:S(2)}, u32[]{:S(2)}) collective-permute-start(bf16[2,256,384]{2,1,0:T(8,128)(2,1)S(1)} %get-tuple-element.15), channel_id=1, source_target_pairs={{0,1},{1,0},{2,3},{3,2},{4,5},{5,4},{6,7},{7,6},{8,9},{9,8},{10,11... | collective-permute-start | bytes 1179656 | tf_op jit(solution)/shard_map/ppermute | solution.py:309

commit v9 on v6

--- a/solution.py
+++ b/solution.py
@@ -204,16 +204,25 @@
             j, 1:2, :
         ]
         all_units.append((gate / (1.0 + jnp.exp(-gate)) * up).astype(jnp.bfloat16))
-    for j in range(w_down.shape[0]):
-        if j == first:
+    total = jnp.zeros((spread.shape[1], w_down.shape[2]), jnp.float32)
+    for start, end in ((0, first), (first, w_down.shape[0])):
+        if start == end:
+            continue
+        if start == first:
             for copy in copies:
                 copy.wait()
-        lines[j * slots : (j + 1) * slots, :] = jnp.dot(
-            all_units[j], held[j][...], preferred_element_type=jnp.float32
-        ).astype(jnp.bfloat16)
-    total = lax.dot_general(
-        spread[...], lines[...], (((0,), (0,)), ((), ())), preferred_element_type=jnp.float32
-    ).astype(jnp.bfloat16)
+        for j in range(start, end):
+            lines[j * slots : (j + 1) * slots, :] = jnp.dot(
+                all_units[j], held[j][...], preferred_element_type=jnp.float32
+            ).astype(jnp.bfloat16)
+        window = slice(start * slots, end * slots)
+        total = total + lax.dot_general(
+            spread[window, :],
+            lines[window, :],
+            (((0,), (0,)), ((), ())),
+            preferred_element_type=jnp.float32,
+        )
+    total = total.astype(jnp.bfloat16)
     out[...] = total.reshape(out.shape)
 
 

time: 46.8 us -> 46.9 us (level)
  no operation moved by 1% of the time
where the time goes in v9:
time: 46.9 us; the launch traced here: 46.7 us
  blocking collectives  30.5 us (65%)
  Pallas kernels  15.6 us (33%)
    all_to_all x1, blocking collectives, body(): lax.all_to_all(outgoing, ('ep', 'tp'), split_axis=0, concat_axis=0, tiled...  17.7 us
    all_to_all x1, blocking collectives, body(): lax.all_to_all(combined, ('ep', 'tp'), split_axis=0, concat_axis=0, tiled...  12.8 us
    pallas_call x1, Pallas kernels, body(): pl.pallas_call(functools.partial(down_kernel, slots), out_shape=jax.Shape...  4.08 us
    pallas_call x1, Pallas kernels, body(): pl.pallas_call(functools.partial(gate_kernel, tp_count, top_count, slots)...  3.95 us
    pallas_call x1, Pallas kernels, body(): pl.pallas_call(functools.partial(up_kernel, slots, counts[0]), out_shape=...  3.8 us
    pallas_call x1, Pallas kernels, body(): pl.pallas_call(functools.partial(prelude_kernel, held_halves, experts, ep...  1.71 us
    pallas_call x1, Pallas kernels, body(): pl.pallas_call(functools.partial(bring_kernel, counts[0] + counts[1]), ou...  1.42 us
  transfers between devices with their start and end apart: 1, of which 1 were waited for; matrix products, arithmetic and copies ran while one was open for 0% of the time, Pallas kernels for 3%

profile of v9, /device:TPU:0, one launch (start us, length us, event | category | flops | bytes accessed | tf_op | source)
XLA Modules:
  0.0 46.7 jit_solution(4073505135420907643)
XLA Ops:
  0.0 0.0 copy-start
  0.0 0.0 slice-start
  0.0 0.0 slice-start.1
  0.0 0.0 slice-start.4
  0.0 1.7 %prelude.1 = bf16[16,4,2176]{2,1,0:T(4,128)(2,1)S(1)} custom-call(bf16[4,4096]{1,0:T(4,128)(2,1)} %refs_0_.1, f32[1,4096]{1,0:T(1,128)} %bitcast.3, f32[64,64]{1,0:T(8,128)} %refs_2_.1, f32[64,64]{1,0:T(8,128)} %refs_3_.1, s32[8,8]{1,0:T(8,128)} %refs_4_.1, f32[8,8]{1,0:T(8,128)} %refs_5_.1), custom_call_target="tpu_custom_call" | custom-call | flops 68719476736 | bytes 1048576 | tf_op jit(solution)/shard_map/prelude/pallas_call | solution.py:266
  1.7 0.0 slice-start.5
  1.8 17.7 %all_to_all.10.received_ref = bf16[16,4,2176]{2,1,0:T(4,128)(2,1)S(1)} all-to-all(bf16[16,4,2176]{2,1,0:T(4,128)(2,1)S(1)} %prelude.1), channel_id=1, replica_groups=mesh['groups'=2,'ep'=8,'tp'=2] {'ep','tp'}, dimensions={0} | all-to-all | bytes 557056 | tf_op jit(solution)/shard_map/all_to_all | solution.py:277
  19.5 0.0 copy-done
  19.5 4.0 %gate.1 = (f32[256,384]{1,0:T(8,128)S(1)}, bf16[256,64]{1,0:T(8,128)(2,1)S(1)}, bf16[256,2048]{1,0:T(8,128)(2,1)S(1)}, bf16[5,384,2048]{2,1,0:T(8,128)(2,1)S(1)}) custom-call(bf16[16,4,2176]{2,1,0:T(4,128)(2,1)S(1)} %all_to_all.10.received_ref, bf16[16,2048,384]{2,1,0:T(8,128)(2,1)S(1)} %copy-done, bf16[16,384,2048]{2,1,0:T(8,128)(2,1)} %w_down.7), custom_call_target="tpu_custom_call" | custom-call | tf_op jit(solution)/shard_map/gate/pallas_call | solution.py:290
  23.5 0.0 slice-done
  23.5 0.0 slice-done.1
  23.5 0.0 slice-done.2
  23.5 0.0 slice-done.3
  23.5 0.0 slice-done.4
  23.5 0.0 slice-done.5
  23.5 3.8 %up.1 = (f32[256,384]{1,0:T(8,128)S(1)}, bf16[2,256,384]{2,1,0:T(8,128)(2,1)S(1)}, bf16[6,384,2048]{2,1,0:T(8,128)(2,1)S(1)}) custom-call(bf16[256,2048]{1,0:T(8,128)(2,1)S(1)} %get-tuple-element.13.inputs, f32[256,384]{1,0:T(8,128)S(1)} %get-tuple-element.12.gate_part, bf16[16,2048,384]{2,1,0:T(8,128)(2,1)S(1)} %bitcast.2, bf16[16,384,2048]{2,1,0:T(8,128)(2,1)} %w_down.7), custom_call_target="tpu_custom_call" | custom-call | tf_op jit(solution)/shard_map/up/pallas_call | solution.py:305
  27.3 0.0 copy-start.1
  27.4 0.2 collective-permute-start
  27.5 1.4 %bring.1.more_2_ = bf16[1,384,2048]{2,1,0:T(8,128)(2,1)S(1)} custom-call(f32[256,384]{1,0:T(8,128)S(1)} %get-tuple-element.14.after.up_part, bf16[16,384,2048]{2,1,0:T(8,128)(2,1)} %w_down.7), custom_call_target="tpu_custom_call" | custom-call | tf_op jit(solution)/shard_map/bring/pallas_call | solution.py:322
  29.0 0.2 collective-permute-done.other
  29.1 0.0 copy-done.1
  29.1 4.1 %down.1 = bf16[16,4,2048]{2,1,0:T(4,128)(2,1)S(1)} custom-call(f32[256,384]{1,0:T(8,128)S(1)} %get-tuple-element.12.gate_part, f32[256,384]{1,0:T(8,128)S(1)} %get-tuple-element.14.after.up_part, bf16[2,256,384]{2,1,0:T(8,128)(2,1)S(1)} %collective-permute-done.other, f32[16,2,384]{2,1,0:T(2,128)S(1)} %copy-done.1, ...), custom_call_target="tpu_custom_call" | custom-call | tf_op jit(solution)/shard_map/down/pallas_call | solution.py:333
  33.2 12.8 %all_to_all.11.returned = bf16[16,4,2048]{2,1,0:T(4,128)(2,1)S(1)} all-to-all(bf16[16,4,2048]{2,1,0:T(4,128)(2,1)S(1)} %down.1), channel_id=1, replica_groups=mesh['groups'=2,'ep'=8,'tp'=2] {'ep','tp'}, dimensions={0} | all-to-all | bytes 524288 | tf_op jit(solution)/shard_map/all_to_all | solution.py:354
  46.0 0.7 %finish.1 = bf16[4,4096]{1,0:T(4,128)(2,1)} custom-call(bf16[16,4,2048]{2,1,0:T(4,128)(2,1)S(1)} %all_to_all.11.returned), custom_call_target="tpu_custom_call" | custom-call | tf_op jit(solution)/shard_map/finish/pallas_call | solution.py:361
  (3 shorter events, 0.0 us)
Async XLA Ops:
  0.0 19.5 %copy-start = (bf16[16,2048,384]{2,1,0:T(8,128)(2,1)S(1)}, bf16[16,2048,384]{2,1,0:T(8,128)(2,1)}, u32[]{:S(2)}) copy-start(bf16[16,2048,384]{2,1,0:T(8,128)(2,1)} %w_gate.1) | copy-start | bytes 75497472
  0.0 23.5 %slice-start = ((s8[25165824]{0:T(1024)(128)(4,1)}), s8[4194304]{0:T(1024)(128)(4,1)S(1)}, s32[]{:S(2)}) async-start(s8[25165824]{0:T(1024)(128)(4,1)} %bitcast.1), calls=%async_computation.2 | async-start | bytes 8388608
  0.0 23.5 %slice-start.1 = ((s8[25165824]{0:T(1024)(128)(4,1)}), s8[4194304]{0:T(1024)(128)(4,1)S(1)}, s32[]{:S(2)}) async-start(s8[25165824]{0:T(1024)(128)(4,1)} %bitcast.1), calls=%async_computation.3 | async-start | bytes 8388608
  0.0 23.5 %slice-start.2 = ((s8[25165824]{0:T(1024)(128)(4,1)}), s8[4194304]{0:T(1024)(128)(4,1)S(1)}, s32[]{:S(2)}) async-start(s8[25165824]{0:T(1024)(128)(4,1)} %bitcast.1), calls=%async_computation.4 | async-start | bytes 8388608
  0.0 23.5 %slice-start.3 = ((s8[25165824]{0:T(1024)(128)(4,1)}), s8[4194304]{0:T(1024)(128)(4,1)S(1)}, s32[]{:S(2)}) async-start(s8[25165824]{0:T(1024)(128)(4,1)} %bitcast.1), calls=%async_computation.5 | async-start | bytes 8388608
  0.0 23.5 %slice-start.4 = ((s8[25165824]{0:T(1024)(128)(4,1)}), s8[4194304]{0:T(1024)(128)(4,1)S(1)}, s32[]{:S(2)}) async-start(s8[25165824]{0:T(1024)(128)(4,1)} %bitcast.1), calls=%async_computation.6 | async-start | bytes 8388608
  1.7 21.8 %slice-start.5 = ((s8[25165824]{0:T(1024)(128)(4,1)}), s8[4194304]{0:T(1024)(128)(4,1)S(1)}, s32[]{:S(2)}) async-start(s8[25165824]{0:T(1024)(128)(4,1)} %bitcast.1), calls=%async_computation.7 | async-start | bytes 8388608
  27.3 1.8 %copy-start.1 = (f32[16,2,384]{2,1,0:T(2,128)S(1)}, f32[16,2,384]{2,1,0:T(2,128)}, u32[]{:S(2)}) copy-start(f32[16,2,384]{2,1,0:T(2,128)} %unit_scales.1) | copy-start | bytes 147460
  27.4 1.8 %collective-permute-start = (bf16[2,256,384]{2,1,0:T(8,128)(2,1)S(1)}, bf16[2,256,384]{2,1,0:T(8,128)(2,1)S(1)}, u32[]{:S(2)}, u32[]{:S(2)}) collective-permute-start(bf16[2,256,384]{2,1,0:T(8,128)(2,1)S(1)} %get-tuple-element.15), channel_id=1, source_target_pairs={{0,1},{1,0},{2,3},{3,2},{4,5},{5,4},{6,7},{7,6},{8,9},{9,8},{10,11... | collective-permute-start | bytes 1179656 | tf_op jit(solution)/shard_map/ppermute | solution.py:318
